TPU v7x, 256 devices: a whole 4x4x8 slice. The times are simulated.
256 devices in a mesh: occ: 16 (over x_lo, z), virt: 16 (over x_hi, y, core).
Axes of the slice: x: 4 (x_hi: 2, x_lo: 2; x = x_hi * 2 + x_lo), y: 4, z: 8, core: 2. Of those that a mesh axis runs over, the one named last changes fastest.
Arguments:
- factors: float32 [128, 512, 512], P('occ'), may hold values from -0.9 to 0.9
- occ_energy: float32 [128], replicated, may hold values from -3 to -0.5
- virt_energy: float32 [512], replicated, may hold values from 0.5 to 9.5
- pairing: int32 [2, 16], replicated, may hold values from 0 to 15, as said below
Outputs:
- pair_energy: float32 [2, 128], P(None, 'occ')
- gradient: float32 [128, 512, 512], P('occ', 'virt')
Inputs may be any that keep to these rules, and one draw needn't show every extreme that they name: `pairing`: in every round each group's partner is another group whose partner is that group.
All inputs are finite; a program needn't handle non-finite values.
Results may differ from a plain program's by a relative error of at most 0.0001.
Values sent between devices are 32-bit elements; how exact they have to be, the bound alone decides.
No kernel may reach another device: no remote copies, remote signals or barrier semaphores. Data moves between devices by JAX's collectives and lax.ppermute only.
A program may use at most 128 MiB of HBM per device.

v0:
```python
import jax
import jax.numpy as jnp
from jax import lax
from jax.sharding import PartitionSpec as P

OG = 8
V = 512


def side_by_side(arrays, axis, split_dim, concat_dim, along):
    both = jnp.concatenate(arrays, axis=along)
    whole, at, gathered = (
        lax.all_to_all(both, axis, split_axis=split_dim, concat_axis=concat_dim, tiled=True),
        0,
        [],
    )
    for a in arrays:
        gathered.append(lax.slice_in_dim(whole, at, at + a.shape[along], axis=along))
        at += a.shape[along]
    return tuple(gathered)


def side_by_side_2(arrays, axis, dim, along):
    ends, at = ([], 0)
    for a in arrays[:-1]:
        at += a.shape[along]
        ends.append(at)
    both = jnp.concatenate(arrays, axis=along)
    return tuple(jnp.split(lax.all_gather(both, axis, axis=dim, tiled=True), ends, axis=along))


def sent_to_all(array, axis):
    copies = jnp.broadcast_to(array, (lax.axis_size(axis), *array.shape))
    return lax.all_to_all(copies, axis, split_axis=0, concat_axis=0, tiled=True)


def over_copies(array, axis):
    everything = sent_to_all(array, axis)
    return jnp.sum(everything, axis=0)


def block_amplitude(
    own_rows, mate_rows, own_piece, fragment, own_energy, mate_energy, energy_left, energy_right
):
    highest = lax.Precision.HIGHEST
    groups_rows, slab_width, naux_width = own_rows.shape
    frag_width = fragment.shape[1]
    contract = (((1,), (1,)), ((), ()))
    coulomb = lax.dot_general(
        own_rows.reshape(groups_rows * slab_width, naux_width),
        fragment.reshape(groups_rows * frag_width, naux_width),
        contract,
        precision=highest,
        preferred_element_type=jnp.float32,
    )
    coulomb = coulomb.reshape(groups_rows, slab_width, groups_rows, frag_width)
    swapped = lax.dot_general(
        own_piece.reshape(groups_rows * frag_width, naux_width),
        mate_rows.reshape(groups_rows * slab_width, naux_width),
        contract,
        precision=highest,
        preferred_element_type=jnp.float32,
    )
    swapped = swapped.reshape(groups_rows, frag_width, groups_rows, slab_width).transpose(
        0, 3, 2, 1
    )
    denominator = (
        energy_left[None, :, None, None]
        + energy_right[None, None, None, :]
        - own_energy[:, None, None, None]
        - mate_energy[None, None, :, None]
    )
    amplitude = -(2.0 * coulomb - swapped) / denominator
    return (amplitude, coulomb)


def block_terms(
    own_rows, mate_rows, own_piece, fragment, own_energy, mate_energy, energy_left, energy_right
):
    highest = lax.Precision.HIGHEST
    groups_rows, slab_width, naux_width = own_rows.shape
    frag_width = fragment.shape[1]
    amplitude, coulomb = block_amplitude(
        own_rows, mate_rows, own_piece, fragment, own_energy, mate_energy, energy_left, energy_right
    )
    energy = jnp.sum(amplitude * coulomb, axis=(1, 2, 3))
    grad_part = jnp.dot(
        amplitude.reshape(groups_rows * slab_width, groups_rows * frag_width),
        fragment.reshape(groups_rows * frag_width, naux_width),
        precision=highest,
        preferred_element_type=jnp.float32,
    )
    return (energy, grad_part)


def per_device(factors, occ_energy, virt_energy, pairing):
    group_index = lax.axis_index("occ")
    column_index = lax.axis_index("virt")
    group_count = lax.axis_size("occ")
    virt_count = lax.axis_size("virt")
    groups_rows, virt_width, naux_width = factors.shape
    slab_width = virt_width // virt_count
    own_rows = lax.dynamic_slice_in_dim(factors, column_index * slab_width, slab_width, 1)
    own_energy = lax.dynamic_slice_in_dim(occ_energy, group_index * groups_rows, groups_rows, 0)
    energy_left = lax.dynamic_slice_in_dim(virt_energy, column_index * slab_width, slab_width, 0)

    def partner_info(round_index):
        partner_row = pairing[round_index]
        mate_index = partner_row[group_index]
        mate_energy = lax.dynamic_slice_in_dim(occ_energy, mate_index * groups_rows, groups_rows, 0)
        return (partner_row, mate_energy)

    first_row, first_energy = partner_info(0)
    second_row, second_energy = partner_info(1)
    split_rows = own_rows.reshape(group_count, groups_rows * slab_width // group_count, naux_width)
    mixed = (
        lax.all_to_all(split_rows, "occ", split_axis=0, concat_axis=0, tiled=True),
        lax.all_to_all(split_rows, "occ", split_axis=0, concat_axis=0, tiled=True),
    )
    arrived = side_by_side(
        (jnp.take(mixed[0], first_row, axis=0), jnp.take(mixed[1], second_row, axis=0)),
        "occ",
        0,
        0,
        1,
    )
    first_mate = arrived[0].reshape(groups_rows, slab_width, naux_width)
    second_mate = arrived[1].reshape(groups_rows, slab_width, naux_width)
    fragments = side_by_side_2((first_mate, second_mate), "virt", 1, 0)
    own_piece = factors
    energy_right = virt_energy
    own_piece, energy_right = (own_piece, energy_right)
    energy_one, grad_one = block_terms(
        own_rows,
        first_mate,
        own_piece,
        fragments[0],
        own_energy,
        first_energy,
        energy_left,
        energy_right,
    )
    energy_two, grad_two = block_terms(
        own_rows,
        second_mate,
        own_piece,
        fragments[1],
        own_energy,
        second_energy,
        energy_left,
        energy_right,
    )
    total_grad, energy_one, energy_two = (grad_one + grad_two, energy_one, energy_two)
    stacked = jnp.stack([energy_one, energy_two])
    stacked = stacked / (V * OG * V)
    pair_energy = over_copies(stacked, "virt")
    return (pair_energy, total_grad.reshape(groups_rows, slab_width, naux_width))


def solution(mesh):
    placed = (P("occ", None, None), P(), P(), P())
    return jax.shard_map(
        per_device,
        mesh=mesh,
        in_specs=placed,
        out_specs=(P(None, "occ"), P("occ", "virt", None)),
        check_vma=False,
    )
```

profile of v0, /device:TPU:1, one launch (start us, length us, event | category | flops | bytes accessed | tf_op | source)
XLA Modules:
  0.0 262.1 jit_solution(2263572044512660959)
XLA Ops:
  7.2 1.9 constant_dynamic-slice_fusion.2
  9.0 10.0 %all-to-all-start = ((f32[16,16,512]{2,1,0:T(8,128)}), f32[16,16,512]{2,1,0:T(8,128)S(1)}, u32[]{:S(2)}, u32[]{:S(2)}) async-start(f32[16,16,512]{2,1,0:T(8,128)} %bitcast.3), calls=%async_computation | async-start | bytes 1048576 | tf_op jit(solution)/shard_map/all_to_all | solution.py:117
  19.1 0.0 all-gather.2.cloned.1.call-start
  19.2 0.8 compare_and_fusion.1
  19.9 12.9 %all-to-all-done = f32[16,16,512]{2,1,0:T(8,128)S(1)} async-done(((f32[16,16,512]{2,1,0:T(8,128)}), f32[16,16,512]{2,1,0:T(8,128)S(1)}, u32[]{:S(2)}, u32[]{:S(2)}) %all-to-all-start) | async-done | bytes 524320 | tf_op jit(solution)/shard_map/all_to_all | solution.py:117
  32.8 0.6 gather_fusion.1
  33.4 0.6 gather_fusion
  34.0 0.1 broadcast_select_fusion
  34.2 0.1 pad_maximum_fusion
  34.3 0.0 copy-start.6
  34.3 0.0 copy-start.7
  34.3 0.0 copy-start.5
  34.3 30.0 %all_to_all.16 = f32[16,32,512]{2,1,0:T(8,128)S(1)} all-to-all(f32[16,32,512]{2,1,0:T(8,128)S(1)} %pad_maximum_fusion), channel_id=1, replica_groups=mesh['occ'=16,'virt'=16] {'occ'}, dimensions={0} | all-to-all | bytes 2097152 | tf_op jit(solution)/shard_map/all_to_all | solution.py:13
  64.3 0.1 fusion.15
  64.4 1.2 pad_maximum_fusion.1
  65.6 0.0 all-gather.2.cloned.1.call-update
  65.6 0.0 copy-done.6
  65.6 0.7 fusion.18
  69.0 0.0 copy-done.7
  69.0 0.1 dynamic_slice.22
  70.4 0.0 copy-done.5
  70.4 0.1 fusion.17
  70.5 0.1 broadcast_add_fusion
  70.6 0.0 slice-start.4
  70.6 0.1 broadcast_subtract_fusion
  70.7 0.0 slice-start.5
  70.7 10.6 %fusion.21 = f32[256,4096]{1,0:T(8,128)S(1)} fusion(f32[256,512]{1,0:T(8,128)S(1)} %bitcast.93, f32[4096,512]{1,0:T(8,128)} %bitcast.78), kind=kOutput, calls=%fused_computation.42 | convolution fusion | flops 6442450944 | bytes 13107200 | tf_op jit(solution)/shard_map/dot_general | solution.py:57
  81.3 5.8 %copy.22 = f32[32,8,8,512]{3,2,1,0:T(8,128)} copy(f32[32,8,8,512]{3,1,2,0:T(8,128)S(1)} %bitcast.85) | data formatting | bytes 8388608
  87.1 0.0 slice-done.4
  87.1 0.0 slice-done.5
  87.1 7.2 %fusion.20 = f32[256,4096]{1,0:T(8,128)S(1)} fusion(f32[256,512]{1,0:T(8,128)S(1)} %bitcast.91, f32[4096,512]{1,0:T(8,128)S(1)} %bitcast.81), kind=kOutput, calls=%fused_computation.41 | convolution fusion | flops 6442450944 | bytes 13107200 | tf_op jit(solution)/shard_map/dot_general | solution.py:57
  94.3 6.1 %copy.21 = f32[32,8,8,512]{3,2,1,0:T(8,128)} copy(f32[32,8,8,512]{3,1,2,0:T(8,128)S(1)} %bitcast.86) | data formatting | bytes 8388608
  100.5 81.0 %all-gather.2.cloned.1.call-done = f32[16,512,512]{2,1,0:T(8,128)} async-done(((f32[16,32,512]{2,1,0:T(8,128)}), f32[16,512,512]{2,1,0:T(8,128)}) %all-gather.2.cloned.1.call-update) | async-done | bytes 16777232 | tf_op jit(solution)/shard_map/all_gather | solution.py:29
  181.5 0.0 copy-start.3
  181.5 0.0 copy-start.4
  181.5 10.0 %fusion = f32[8,32,8,512]{3,1,2,0:T(8,128)S(1)} fusion(f32[8,32,512]{2,1,0:T(8,128)} %constant_dynamic-slice_fusion.2, f32[16,512,512]{2,1,0:T(8,128)} %all-gather.2.cloned.1.call-done), kind=kOutput, calls=%fused_computation.2 | convolution fusion | flops 6442450944 | bytes 13107200 | tf_op jit(solution)/shard_map/dot_general | solution.py:49
  191.5 0.0 copy-done.3
  191.5 0.0 copy-done.4
  191.6 16.4 %multiply_reduce_fusion.1 = (f32[8]{0:T(128)S(1)}, f32[8,32,8,512]{3,1,2,0:T(8,128)}, f32[8]{0:T(128)S(1)}, f32[8,32,8,512]{3,1,2,0:T(8,128)}) fusion(f32[8]{0:T(128)S(1)} %get-tuple-element.21, f32[8,32,512]{2,1,0:T(8,128)S(1)} %broadcast_subtract_fusion, f32[8,512,8,32]{1,0,3,2:T(8,128)S(1)} %bitcast.95, f32[8,32,8,512]{3,1,2,0:T(8,128)S(1)} %fusion, ...), kind=kOutput, calls=%fused_computation.13 | convolution fusion | flops 6457131008 | bytes 30408832 | tf_op jit(solution)/shard_map/dot_general | solution.py:49
  208.0 0.6 broadcast_in_dim.11
  208.6 3.7 %all-to-all-start.2 = ((f32[16,2,8]{2,1,0:T(2,128)}), f32[16,2,8]{2,1,0:T(2,128)S(1)}, u32[]{:S(2)}, u32[]{:S(2)}) async-start(f32[16,2,8]{2,1,0:T(2,128)} %broadcast_in_dim.11), calls=%async_computation.2 | async-start | bytes 32768 | tf_op jit(solution)/shard_map/all_to_all | solution.py:34
  212.3 0.0 slice-start
  212.3 4.8 %copy.17 = f32[8,32,8,512]{3,2,1,0:T(8,128)S(1)} copy(f32[8,32,8,512]{3,1,2,0:T(8,128)} %get-tuple-element.4) | data formatting | bytes 8388608 | tf_op jit(solution)/shard_map/div | solution.py:73
  217.1 0.0 slice-start.1
  217.1 0.0 copy-start.2
  217.1 3.9 %copy.23 = f32[32,8,8,512]{3,1,2,0:T(8,128)S(1)} copy(f32[32,8,8,512]{3,2,1,0:T(8,128)S(1)} %bitcast.88) | data formatting | bytes 8388608
  221.0 0.0 slice-start.2
  221.0 0.0 copy-done.2
  221.0 2.4 copy.18
  223.5 0.0 slice-start.3
  223.5 6.0 %copy.24 = f32[32,8,8,512]{3,1,2,0:T(8,128)} copy(f32[32,8,8,512]{3,2,1,0:T(8,128)S(1)} %bitcast.89) | data formatting | bytes 8388608
  229.5 0.0 slice-done
  229.5 0.0 slice-done.1
  229.5 0.0 slice-done.2
  229.5 0.0 slice-done.3
  229.5 6.8 %fusion.14 = (f32[8,512,512]{2,1,0:T(8,128)}, f32[8,512,512]{2,1,0:T(8,128)}) fusion(f32[16,512,512]{2,1,0:T(8,128)S(1)} %bitcast.77), kind=kLoop, calls=%fused_computation.35 | loop fusion | bytes 33554432 | tf_op jit(solution)/shard_map/split | solution.py:29
  236.3 0.0 copy-start
  236.3 0.0 copy-start.1
  236.3 10.1 %fusion.22 = f32[256,512]{1,0:T(8,128)S(1)} fusion(f32[256,4096]{1,0:T(8,128)S(1)} %bitcast.84, f32[4096,512]{1,0:T(8,128)} %bitcast.82), kind=kOutput, calls=%fused_computation.43 | convolution fusion | flops 6442450944 | bytes 13107200 | tf_op jit(solution)/shard_map/dot_general | solution.py:87
  246.4 0.0 copy-done
  246.4 0.0 copy-done.1
  246.4 8.0 %convolution_add_fusion = f32[256,512]{1,0:T(8,128)} fusion(f32[256,512]{1,0:T(8,128)S(1)} %fusion.22, f32[256,4096]{1,0:T(8,128)S(1)} %bitcast.87, f32[4096,512]{1,0:T(8,128)S(1)} %bitcast.83), kind=kOutput, calls=%fused_computation.14 | convolution fusion | flops 6442582016 | bytes 13631488 | tf_op jit(solution)/shard_map/dot_general | solution.py:87
  254.4 0.0 all-to-all-done.2
  254.4 0.6 reduce_sum.29
  (6 shorter events, 0.0 us)
Async XLA Ops:
  9.0 23.8 %all-to-all-start = ((f32[16,16,512]{2,1,0:T(8,128)}), f32[16,16,512]{2,1,0:T(8,128)S(1)}, u32[]{:S(2)}, u32[]{:S(2)}) async-start(f32[16,16,512]{2,1,0:T(8,128)} %bitcast.3), calls=%async_computation | async-start | bytes 1048576 | tf_op jit(solution)/shard_map/all_to_all | solution.py:117
  19.1 162.4 %all-gather.2.cloned.1.call-start = ((), (), s32[]{:S(2)}) async-start(), calls=%async_computation.3 | async-start | bytes 17825792 | tf_op jit(solution)/shard_map/all_gather | solution.py:29
  34.3 31.3 %copy-start.6 = (s32[2,16]{1,0:T(2,128)S(1)}, s32[2,16]{1,0:T(2,128)}, u32[]{:S(2)}) copy-start(s32[2,16]{1,0:T(2,128)} %param.9) | copy-start | bytes 388
  34.3 34.7 %copy-start.7 = (f32[512]{0:T(512)S(1)}, f32[512]{0:T(512)}, u32[]{:S(2)}) copy-start(f32[512]{0:T(512)} %param.8) | copy-start | bytes 6148
  34.3 36.1 %copy-start.5 = (f32[128]{0:T(128)S(1)}, f32[128]{0:T(128)}, u32[]{:S(2)}) copy-start(f32[128]{0:T(128)} %param.7) | copy-start | bytes 1540
  70.6 16.5 %slice-start.4 = ((s8[8388608]{0:T(1024)(128)(4,1)}), s8[4194304]{0:T(1024)(128)(4,1)S(1)}, s32[]{:S(2)}) async-start(s8[8388608]{0:T(1024)(128)(4,1)} %bitcast.79), calls=%async_computation.8 | async-start | bytes 8388608
  70.7 16.4 %slice-start.5 = ((s8[8388608]{0:T(1024)(128)(4,1)}), s8[4194304]{0:T(1024)(128)(4,1)S(1)}, s32[]{:S(2)}) async-start(s8[8388608]{0:T(1024)(128)(4,1)} %bitcast.79), calls=%async_computation.9 | async-start | bytes 8388608
  181.5 10.0 %copy-start.3 = (f32[32,8,8,512]{3,2,1,0:T(8,128)S(1)}, f32[32,8,8,512]{3,2,1,0:T(8,128)}, u32[]{:S(2)}) copy-start(f32[32,8,8,512]{3,2,1,0:T(8,128)} %copy.22) | copy-start | bytes 12582916
  181.5 10.0 %copy-start.4 = (f32[32,8,8,512]{3,2,1,0:T(8,128)S(1)}, f32[32,8,8,512]{3,2,1,0:T(8,128)}, u32[]{:S(2)}) copy-start(f32[32,8,8,512]{3,2,1,0:T(8,128)} %copy.21) | copy-start | bytes 12582916
  208.6 45.8 %all-to-all-start.2 = ((f32[16,2,8]{2,1,0:T(2,128)}), f32[16,2,8]{2,1,0:T(2,128)S(1)}, u32[]{:S(2)}, u32[]{:S(2)}) async-start(f32[16,2,8]{2,1,0:T(2,128)} %broadcast_in_dim.11), calls=%async_computation.2 | async-start | bytes 32768 | tf_op jit(solution)/shard_map/all_to_all | solution.py:34
  212.3 17.2 %slice-start = ((s8[16777216]{0:T(1024)(128)(4,1)}), s8[4194304]{0:T(1024)(128)(4,1)S(1)}, s32[]{:S(2)}) async-start(s8[16777216]{0:T(1024)(128)(4,1)} %bitcast.76), calls=%async_computation.4 | async-start | bytes 8388608
  217.1 12.4 %slice-start.1 = ((s8[16777216]{0:T(1024)(128)(4,1)}), s8[4194304]{0:T(1024)(128)(4,1)S(1)}, s32[]{:S(2)}) async-start(s8[16777216]{0:T(1024)(128)(4,1)} %bitcast.76), calls=%async_computation.5 | async-start | bytes 8388608
  217.1 3.9 %copy-start.2 = (f32[8,32,8,512]{3,1,2,0:T(8,128)S(1)}, f32[8,32,8,512]{3,1,2,0:T(8,128)}, u32[]{:S(2)}) copy-start(f32[8,32,8,512]{3,1,2,0:T(8,128)} %get-tuple-element.16) | copy-start | bytes 12582916
  221.0 8.5 %slice-start.2 = ((s8[16777216]{0:T(1024)(128)(4,1)}), s8[4194304]{0:T(1024)(128)(4,1)S(1)}, s32[]{:S(2)}) async-start(s8[16777216]{0:T(1024)(128)(4,1)} %bitcast.76), calls=%async_computation.6 | async-start | bytes 8388608
  223.5 6.0 %slice-start.3 = ((s8[16777216]{0:T(1024)(128)(4,1)}), s8[4194304]{0:T(1024)(128)(4,1)S(1)}, s32[]{:S(2)}) async-start(s8[16777216]{0:T(1024)(128)(4,1)} %bitcast.76), calls=%async_computation.7 | async-start | bytes 8388608
  236.3 10.2 %copy-start = (f32[8,512,512]{2,1,0:T(8,128)S(1)}, f32[8,512,512]{2,1,0:T(8,128)}, u32[]{:S(2)}) copy-start(f32[8,512,512]{2,1,0:T(8,128)} %get-tuple-element.11) | copy-start | bytes 25165828
  236.3 10.2 %copy-start.1 = (f32[32,8,8,512]{3,1,2,0:T(8,128)S(1)}, f32[32,8,8,512]{3,1,2,0:T(8,128)}, u32[]{:S(2)}) copy-start(f32[32,8,8,512]{3,1,2,0:T(8,128)} %copy.24) | copy-start | bytes 12582916
Sparse Core Ops, SparseCore 0:
  65.7 115.7 all-gather.1
where the time goes:
time: 266 us; the launch traced here: 262 us
  waiting for transfers between devices  94 us (35%)
  matrix products  62.4 us (23%)
  local copies, waits for them, and re-layouts  39.8 us (15%)
  blocking collectives  30 us (11%)
  between operations  18.6 us (7%)
  starting transfers between devices  13.8 us (5%)
  other arithmetic  3.62 us (1%)
    all_gather x1, waiting for transfers between devices, side_by_side_2(): lax.all_gather(both, axis, axis=dim, tiled=True)  81 us
    all_to_all x1, blocking collectives, side_by_side(): lax.all_to_all(both, axis, split_axis=split_dim, concat_axis=concat_dim,...  30 us
    dot_general x2, matrix products, block_amplitude(): lax.dot_general(own_rows.reshape(groups_rows * slab_width, naux_width), f...  26.4 us
    unnamed x32, local copies, waits for them, and re-layouts  21.9 us
    dot_general x2, matrix products, block_terms(): jnp.dot(amplitude.reshape(groups_rows * slab_width, groups_rows * frag_wi...  18.1 us
    dot_general x2, matrix products, block_amplitude(): lax.dot_general(own_piece.reshape(groups_rows * frag_width, naux_width),...  17.8 us
    all_to_all x1, waiting for transfers between devices, per_device(): lax.all_to_all(split_rows, 'occ', split_axis=0, concat_axis=0, tiled=True)  12.9 us
    all_to_all x1, starting transfers between devices, per_device(): lax.all_to_all(split_rows, 'occ', split_axis=0, concat_axis=0, tiled=True)  10 us
  transfers between devices with their start and end apart: 3, of which 2 were waited for; matrix products, arithmetic and copies ran while one was open for 28% of the time, Pallas kernels for 0%

commit v1 on v0

v1 whole, which is shorter than its diff:
```python
import jax
import jax.numpy as jnp
from jax import lax
from jax.experimental import pallas as pl
from jax.experimental.pallas import tpu as pltpu
from jax.sharding import PartitionSpec as P

OG = 8
V = 512
NAUX = 512
ROUNDS = 2
GROUPS = 16
COLS = 16
HALF = V // 2
PIECE = OG * V // COLS
PART = PIECE // GROUPS
SLAB = V // COLS
ROWS = SLAB * NAUX // 128
VMEM_LIMIT = 16 << 20


CORE, OTHERS = 1, (8, 2)


def swap(array, flip):
    return lax.ppermute(array, "virt", [(v, v ^ flip) for v in range(COLS)])


def split(x):
    high = x.astype(jnp.bfloat16)
    return high, (x - high.astype(jnp.float32)).astype(jnp.bfloat16)


def dot(x, y, y_dim):
    return lax.dot_general(x, y, (((1,), (y_dim,)), ((), ())), preferred_element_type=jnp.float32)


def at(half, parity):
    return pl.ds(pl.multiple_of((half + parity - 2 * half * parity) * HALF, HALF), HALF)


def call(kernel, out_shape, name, args, scratch=(), scalars=0, cost=None):
    vmem = pl.BlockSpec(memory_space=pltpu.VMEM)
    smem = pl.BlockSpec(memory_space=pltpu.SMEM)
    many = isinstance(out_shape, tuple)
    return pl.pallas_call(
        kernel,
        out_shape=out_shape,
        in_specs=[smem] * scalars + [vmem] * (len(args) - scalars),
        out_specs=(vmem,) * len(out_shape) if many else vmem,
        scratch_shapes=scratch,
        compiler_params=pltpu.CompilerParams(vmem_limit_bytes=VMEM_LIMIT),
        cost_estimate=cost,
        name=name,
    )(*args)


def shape(*dims, dtype=jnp.float32):
    return jax.ShapeDtypeStruct(dims, dtype)


def halves_kernel(place_ref, own_ref, out_ref):
    for k in range(2):
        for h in range(2):
            high, low = split(own_ref[k, at(h, place_ref[0]), :])
            out_ref[k, h * HALF : (h + 1) * HALF, :] = high
            out_ref[k, V + h * HALF : V + (h + 1) * HALF, :] = low


def pick_kernel(mates_ref, mixed_ref, out_ref):
    for g in range(GROUPS):
        for r in range(ROUNDS):
            out_ref[g, r * PART : (r + 1) * PART, :] = mixed_ref[mates_ref[r, g]]


def cut_kernel(both_ref, *out_refs):
    for g in range(GROUPS):
        for r in range(ROUNDS):
            out_refs[r][g * PART : (g + 1) * PART, :] = both_ref[g, r * PART : (r + 1) * PART, :]


def unit_kernel(number, last, place_ref, occ_ref, own_ref, near_ref, far_ref, *rest):
    column_ref, row_ref = rest[:2]
    before_ref = rest[2] if number > 0 else None
    energy_refs = rest[3:6] if last else ()
    scratch = rest[-6:]
    high, low = scratch[:2]
    coulombs, amplitudes = scratch[2:4], scratch[4:]
    grad_ref = rest[-7] if last else rest[-8]
    for h, ref in enumerate((near_ref, far_ref)):
        s = slice(h * HALF, (h + 1) * HALF)
        high[s, :], low[s, :] = split(ref[...])

    def coulomb(n):
        own = own_ref.at[n]
        for b in range(2):
            s = slice(b * HALF, (b + 1) * HALF)
            both = dot(own[...], high[s, :], 1)
            coulombs[n][:, s] = both[:V] + (both[V:] + dot(own[:V, :], low[s, :], 1))

    def amplitude(n):
        shift = occ_ref[place_ref[1 + n]] + occ_ref[place_ref[3 + number]]
        total = jnp.zeros((8, HALF), jnp.float32)
        for a in range(2):
            s = slice(a * HALF, (a + 1) * HALF)
            for b in range(2):
                t = slice(b * HALF, (b + 1) * HALF)
                here = coulombs[n][s, t]
                below = column_ref[s, :] + row_ref[:, t] - shift
                value = (coulombs[n][t, s].T - 2.0 * here) / below
                total = total + jnp.sum((value * here).reshape(HALF // 8, 8, HALF), axis=0)
                value_high, value_low = split(value)
                amplitudes[n][s, t] = value_high
                amplitudes[n][V + a * HALF : V + (a + 1) * HALF, t] = value_low
        return total[:, :128] + total[:, 128:]

    def gradient(n):
        for p in range(2):
            s = slice(p * HALF, (p + 1) * HALF)
            both = dot(amplitudes[n][...], high[:, s], 0)
            value = both[:V] + (both[V:] + dot(amplitudes[n][:V, :], low[:, s], 0))
            if before_ref is not None:
                value = value + before_ref[n, :, s]
            if not last:
                grad_ref[n, :, s] = value
                continue
            for t in range(COLS):
                to = t + place_ref[0] * (COLS // 2)
                to = to - jnp.where(to >= COLS, COLS, 0)
                for e in range(SLAB // 8):
                    for q in range(HALF // 128):
                        line = n * ROWS + (e * 4 + p * 2 + q) * 8
                        grad_ref[to, line : line + 8, :] = value[
                            t * SLAB + e * 8 : t * SLAB + e * 8 + 8, q * 128 : (q + 1) * 128
                        ]

    energies = []
    coulomb(0)
    coulomb(1)
    for n in range(2):
        energies.append(amplitude(n))
        gradient(n)
    if not last:
        for n in range(2):
            rest[-7][n] = energies[n]
        return
    line = lax.broadcasted_iota(jnp.int32, (8, 128), 0)
    table = jnp.zeros((8, 128), jnp.float32)
    for n in range(2):
        for r, value in (
            (0, energy_refs[0][n] + energy_refs[2][n]),
            (1, energy_refs[1][n] + energies[n]),
        ):
            table = jnp.where(line == 2 * r + n, jnp.sum(value, axis=0, keepdims=True), table)
    for t in range(COLS):
        grad_ref[t, 2 * ROWS :, :] = table


def unit(number, place, occ, own, near, far, column, row, before, energies=()):
    last = len(energies) > 0
    args = [place, occ, own, near, far, column, row]
    args += ([] if before is None else [before]) + list(energies)

    def body(*refs):
        unit_kernel(number, last, *refs)

    out = shape(COLS, 2 * ROWS + 8, 128)
    return call(
        body,
        out if last else (shape(2, V, NAUX), shape(2, 8, 128)),
        "unit",
        args,
        scratch=[pltpu.VMEM((V, NAUX), jnp.bfloat16)] * 2
        + [pltpu.VMEM((V, V), jnp.float32)] * 2
        + [pltpu.VMEM((2 * V, V), jnp.bfloat16)] * 2,
        scalars=2,
        cost=pl.CostEstimate(
            flops=24 * V * V * NAUX, bytes_accessed=16 * V * NAUX, transcendentals=0
        ),
    )


def finish_kernel(slabs_ref, grad_ref, energy_ref):
    line = lax.broadcasted_iota(jnp.int32, (8, 128), 0)
    lane = lax.broadcasted_iota(jnp.int32, (8, 128), 1)
    table = jnp.zeros((8, 128), jnp.float32)

    def added(sources, rows):
        values = [slabs_ref[s, rows, :] for s in sources]
        return (values[0] + values[1]) + (values[2] + values[3])

    for quad in range(2):
        for core in range(2):
            sources = [(quad ^ (y & 1)) * 8 + y * 2 + core for y in range(4)]
            energy = jnp.sum(added(sources, slice(2 * ROWS, 2 * ROWS + 8)), axis=1, keepdims=True)
            for n in range(2):
                i = quad * 4 + core * 2 + n
                for p in range(4):
                    for q in range(4):
                        at_row = n * ROWS + (4 * p + q) * 8
                        grad_ref[i, 8 * p : 8 * p + 8, q * 128 : (q + 1) * 128] = added(
                            sources, slice(at_row, at_row + 8)
                        )
                for r in range(ROUNDS):
                    value = energy[2 * r + n : 2 * r + n + 1]
                    table = jnp.where((line == r) & (lane == i), value, table)
    energy_ref[...] = table[:ROUNDS, :OG] * (1.0 / (V * OG * V))


def per_device(factors, occ_energy, virt_energy, pairing):
    group = lax.axis_index("occ")
    v = lax.axis_index("virt")
    core = v & 1
    y = (v >> 1) & 3
    x = v >> 3
    slab = lax.dynamic_slice_in_dim(factors.reshape(OG * V, NAUX), v * PIECE, PIECE, 0)
    mixed = lax.all_to_all(
        slab.reshape(GROUPS, PART, NAUX), "occ", split_axis=0, concat_axis=0, tiled=True
    )
    orbital = (x ^ (y & 1)) * 4 + core * 2
    mates = [pairing[r, group] * OG for r in range(ROUNDS)]
    j = x * 4 + y
    place = jnp.stack(
        [core, group * OG + orbital, group * OG + orbital + 1]
        + [mates[0] + j, mates[1] + j, mates[0] + (j ^ 4), mates[1] + (j ^ 1)]
    ).astype(jnp.int32)
    turned = lax.dynamic_slice_in_dim(
        jnp.concatenate([virt_energy, virt_energy]), core * HALF, V, 0
    )
    column, row = turned.reshape(V, 1), turned.reshape(1, V)
    own = call(
        halves_kernel,
        shape(2, 2 * V, NAUX, dtype=jnp.bfloat16),
        "halves",
        [place, lax.dynamic_slice_in_dim(factors, orbital, 2, 0)],
        scalars=1,
    )
    mixed, own, place, column, row = lax.optimization_barrier((mixed, own, place, column, row))
    picked = call(
        pick_kernel, shape(GROUPS, ROUNDS * PART, NAUX), "pick", [pairing, mixed], scalars=1
    )
    both = lax.all_to_all(picked, "occ", split_axis=0, concat_axis=0, tiled=True)
    pieces = call(cut_kernel, (shape(PIECE, NAUX),) * ROUNDS, "cut", [both])
    others = [swap(piece, flip) for piece, flip in zip(pieces, OTHERS)]
    grads, energies = None, []
    for r in range(ROUNDS):
        near, far = pieces[r], swap(pieces[r], CORE)
        grads, energy = unit(r, place, occ_energy, own, near, far, column, row, grads)
        energies.append(energy)
    *others, grads = lax.optimization_barrier((*others, grads))
    near, far = others[0], swap(others[0], CORE)
    grads, energy = unit(2, place, occ_energy, own, near, far, column, row, grads)
    energies.append(energy)
    near, far = others[1], swap(others[1], CORE)
    sent = unit(3, place, occ_energy, own, near, far, column, row, grads, energies)
    slabs = lax.all_to_all(sent, "virt", split_axis=0, concat_axis=0, tiled=True)
    gradient, pair_energy = call(
        finish_kernel, (shape(OG, SLAB, NAUX), shape(ROUNDS, OG)), "finish", [slabs]
    )
    return (pair_energy, gradient)


def solution(mesh):
    placed = (P("occ", None, None), P(), P(), P())
    return jax.shard_map(
        per_device,
        mesh=mesh,
        in_specs=placed,
        out_specs=(P(None, "occ"), P("occ", "virt", None)),
        check_vma=False,
    )
```

time: 266 us -> 125 us (0.47); the launches traced: 262 us -> 124 us
  waiting for transfers between devices: 94 us -> 12.3 us
  matrix products: 62.4 us -> 0 us
  blocking collectives: 30 us -> 65.6 us
  local copies, waits for them, and re-layouts: 39.8 us -> 4.63 us
  Pallas kernels: 0 us -> 20.9 us
  between operations: 18.6 us -> 2.13 us
  starting transfers between devices: 13.8 us -> 18.7 us
  other arithmetic: 3.62 us -> 0.01 us
    all_gather x1 -> x0, waiting for transfers between devices: 81 us -> none  [side_by_side_2(): lax.all_gather(both, axis, axis=dim, tiled=True)]
    dot_general x6 -> x0, matrix products: 62.4 us -> none  [the longest x2 26.4 us: block_amplitude(): lax.dot_general(own_rows.reshape(groups_rows * slab_width, naux_width), f...]
    all_to_all x1 -> x2, blocking collectives: 30 us -> 65.6 us  [the longest x1 35.7 us: per_device(): lax.all_to_all(sent, 'virt', split_axis=0, concat_axis=0, tiled=True)]
    unnamed x32 -> x6, local copies, waits for them, and re-layouts: 21.9 us -> 0.02 us
    pallas_call x0 -> x8, Pallas kernels: none -> 20.9 us  [call(): pl.pallas_call(kernel, out_shape=out_shape, in_specs=[smem] * scalars + [...]
    ppermute x0 -> x6, starting transfers between devices: none -> 8.7 us  [swap(): return lax.ppermute(array, 'virt', [(v, v ^ flip) for v in range(COLS)])]
    div x2 -> x0, local copies, waits for them, and re-layouts: 7.21 us -> none  [block_amplitude(): amplitude = -(2.0 * coulomb - swapped) / denominator]
    split x1 -> x0, local copies, waits for them, and re-layouts: 6.78 us -> none  [side_by_side_2(): jnp.split(lax.all_gather(both, axis, axis=dim, tiled=True), ends, axis=al...]
  transfers between devices with their start and end apart: 3 -> 7, of which waited for: 2 -> 4; matrix products, arithmetic and copies ran while one was open for 28% -> 2% of each run, Pallas kernels for 0% -> 12%
where the time goes in v1:
time: 125 us; the launch traced here: 124 us
  blocking collectives  65.6 us (52%)
  Pallas kernels  20.9 us (17%)
  starting transfers between devices  18.7 us (15%)
  waiting for transfers between devices  12.3 us (10%)
  local copies, waits for them, and re-layouts  4.63 us (4%)
  between operations  2.13 us (2%)
    all_to_all x1, blocking collectives, per_device(): lax.all_to_all(sent, 'virt', split_axis=0, concat_axis=0, tiled=True)  35.7 us
    all_to_all x1, blocking collectives, per_device(): lax.all_to_all(picked, 'occ', split_axis=0, concat_axis=0, tiled=True)  29.9 us
    pallas_call x8, Pallas kernels, call(): pl.pallas_call(kernel, out_shape=out_shape, in_specs=[smem] * scalars + [...  20.9 us
    all_to_all x1, starting transfers between devices, per_device(): lax.all_to_all(slab.reshape(GROUPS, PART, NAUX), 'occ', split_axis=0, con...  10 us
    all_to_all x1, waiting for transfers between devices, per_device(): lax.all_to_all(slab.reshape(GROUPS, PART, NAUX), 'occ', split_axis=0, con...  8.8 us
    ppermute x6, starting transfers between devices, swap(): return lax.ppermute(array, 'virt', [(v, v ^ flip) for v in range(COLS)])  8.7 us
    ppermute x6, waiting for transfers between devices, swap(): return lax.ppermute(array, 'virt', [(v, v ^ flip) for v in range(COLS)])  3.52 us
  transfers between devices with their start and end apart: 7, of which 4 were waited for; matrix products, arithmetic and copies ran while one was open for 2% of the time, Pallas kernels for 12%

profile of v1, /device:TPU:1, one launch (start us, length us, event | category | flops | bytes accessed | tf_op | source)
XLA Modules:
  0.0 124.3 jit_solution(6724695518431902810)
XLA Ops:
  0.6 0.0 copy-start
  0.6 1.9 %constant_dynamic-slice_fusion.2 = f32[256,512]{1,0:T(8,128)} fusion(f32[4096,512]{1,0:T(8,128)} %bitcast.18, s32[]{:T(128)S(6)} %select_n.13), kind=kLoop, calls=%fused_computation.3 | loop fusion | bytes 1048580 | tf_op jit(solution)/shard_map/dynamic_slice | solution.py:216
  2.5 10.0 %all-to-all-start = ((f32[16,16,512]{2,1,0:T(8,128)}), f32[16,16,512]{2,1,0:T(8,128)S(1)}, u32[]{:S(2)}, u32[]{:S(2)}) async-start(f32[16,16,512]{2,1,0:T(8,128)} %bitcast.1), calls=%async_computation | async-start | bytes 1048576 | tf_op jit(solution)/shard_map/all_to_all | solution.py:217
  12.6 0.0 copy-done
  12.6 0.7 constant_dynamic-slice_fusion.3
  14.6 0.1 stack.31.place_ref.refs_0_
  14.7 1.8 %constant_dynamic-slice_fusion.own_ref = f32[2,512,512]{2,1,0:T(8,128)S(1)} fusion(f32[8,512,512]{2,1,0:T(8,128)} %param.4, s32[]{:T(128)S(6)} %select_n.15), kind=kLoop, calls=%fused_computation.1 | loop fusion | bytes 4194308 | tf_op jit(solution)/shard_map/dynamic_slice | solution.py:235
  16.5 0.0 copy-start.2
  16.5 0.9 halves.1.refs_2_
  17.4 0.0 copy-done.2
  17.4 0.1 dynamic_slice.19
  17.5 8.8 %all-to-all-done.mixed_ref = f32[16,16,512]{2,1,0:T(8,128)S(1)} async-done(((f32[16,16,512]{2,1,0:T(8,128)}), f32[16,16,512]{2,1,0:T(8,128)S(1)}, u32[]{:S(2)}, u32[]{:S(2)}) %all-to-all-start) | async-done | bytes 524320 | tf_op jit(solution)/shard_map/all_to_all | solution.py:217
  26.3 0.6 pick.1
  26.9 0.0 copy-start.1
  27.0 29.9 %all_to_all.15.both_ref = f32[16,32,512]{2,1,0:T(8,128)S(1)} all-to-all(f32[16,32,512]{2,1,0:T(8,128)S(1)} %pick.1), channel_id=1, replica_groups=mesh['occ'=16,'virt'=16] {'occ'}, dimensions={0} | all-to-all | bytes 2097152 | tf_op jit(solution)/shard_map/all_to_all | solution.py:242
  56.8 0.9 cut.1
  57.7 3.2 %collective-permute-start.3 = (f32[256,512]{1,0:T(8,128)}, f32[256,512]{1,0:T(8,128)}, u32[]{:S(2)}, u32[]{:S(2)}) collective-permute-start(f32[256,512]{1,0:T(8,128)} %get-tuple-element.23.refs_3_), channel_id=1, source_target_pairs={{0,1},{1,0},{2,3},{3,2},{4,5},{5,4},{6,7},{7,6},{8,9},{9,8},{10,11... | collective-permute-start | bytes 1572872 | tf_op jit(solution)/shard_map/ppermute | solution.py:26
  60.9 0.0 collective-permute-start.2
  60.9 0.1 copy.7.refs_5_
  61.0 2.5 %collective-permute-start = (f32[256,512]{1,0:T(8,128)}, f32[256,512]{1,0:T(8,128)S(1)}, u32[]{:S(2)}, u32[]{:S(2)}) collective-permute-start(f32[256,512]{1,0:T(8,128)} %get-tuple-element.23.refs_3_), channel_id=1, source_target_pairs={{0,8},{1,9},{2,10},{3,11},{4,12},{5,13},{6,14},{7,15},{8,0},{9,1},... | collective-permute-start | bytes 1572872 | tf_op jit(solution)/shard_map/ppermute | solution.py:26
  63.6 1.3 %collective-permute-start.1 = (f32[256,512]{1,0:T(8,128)S(1)}, f32[256,512]{1,0:T(8,128)S(1)}, u32[]{:S(2)}, u32[]{:S(2)}) collective-permute-start(f32[256,512]{1,0:T(8,128)S(1)} %get-tuple-element.24.refs_3_), channel_id=1, source_target_pairs={{0,2},{1,3},{2,0},{3,1},{4,6},{5,7},{6,4},{7,5},{8,10},{9,11},{10,... | collective-permute-start | bytes 1572872 | tf_op jit(solution)/shard_map/ppermute | solution.py:26
  64.9 0.0 collective-permute-done.3.refs_4_
  64.9 0.0 copy-done.1
  64.9 4.8 %unit.4 = (f32[2,512,512]{2,1,0:T(8,128)S(1)}, f32[2,8,128]{2,1,0:T(8,128)S(1)}) custom-call(s32[7]{0:T(128)S(1)} %stack.31.place_ref.refs_0_, f32[128]{0:T(128)S(1)} %copy-done.1, bf16[2,1024,512]{2,1,0:T(8,128)(2,1)S(1)} %halves.1.refs_2_, f32[256,512]{1,0:T(8,128)} %get-tuple-element.23.refs_3_, f32[256,512]{1,0:T(8,128)} %collective-permute-done.3.refs_4_, ...), custom_call_target="tpu_custom_call" | custom-call | flops 3221225472 | bytes 4194304 | tf_op jit(solution)/shard_map/unit/pallas_call | solution.py:46
  69.6 0.0 collective-permute-done.2.refs_4_
  69.6 4.6 %unit.5 = (f32[2,512,512]{2,1,0:T(8,128)S(1)}, f32[2,8,128]{2,1,0:T(8,128)S(1)}) custom-call(s32[7]{0:T(128)S(1)} %stack.31.place_ref.refs_0_, f32[128]{0:T(128)S(1)} %copy-done.1, bf16[2,1024,512]{2,1,0:T(8,128)(2,1)S(1)} %halves.1.refs_2_, f32[256,512]{1,0:T(8,128)S(1)} %get-tuple-element.24.refs_3_, f32[256,512]{1,0:T(8,128)} %collective-permute-done.2.refs_4_, ...), custom_call_target="tpu_custom_call" | custom-call | flops 3221225472 | bytes 4194304 | tf_op jit(solution)/shard_map/unit/pallas_call | solution.py:46
  74.2 1.6 %collective-permute-done.refs_3_ = f32[256,512]{1,0:T(8,128)S(1)} collective-permute-done((f32[256,512]{1,0:T(8,128)}, f32[256,512]{1,0:T(8,128)S(1)}, u32[]{:S(2)}, u32[]{:S(2)}) %collective-permute-start) | collective-permute-done | bytes 524320 | tf_op jit(solution)/shard_map/ppermute | solution.py:26
  75.8 0.4 collective-permute-done.1.refs_3_
  76.2 1.7 %collective-permute-start.5 = (f32[256,512]{1,0:T(8,128)S(1)}, f32[256,512]{1,0:T(8,128)S(1)}, u32[]{:S(2)}, u32[]{:S(2)}) collective-permute-start(f32[256,512]{1,0:T(8,128)S(1)} %collective-permute-done.refs_3_), channel_id=1, source_target_pairs={{0,1},{1,0},{2,3},{3,2},{4,5},{5,4},{6,7},{7,6},{8,9},{9,8},{10,11... | collective-permute-start | bytes 1572872 | tf_op jit(solution)/shard_map/ppermute | solution.py:26
  77.9 0.0 collective-permute-start.4
  77.9 1.5 %collective-permute-done.5.refs_4_ = f32[256,512]{1,0:T(8,128)S(1)} collective-permute-done((f32[256,512]{1,0:T(8,128)S(1)}, f32[256,512]{1,0:T(8,128)S(1)}, u32[]{:S(2)}, u32[]{:S(2)}) %collective-permute-start.5) | collective-permute-done | bytes 524320 | tf_op jit(solution)/shard_map/ppermute | solution.py:26
  79.4 4.1 %unit.6 = (f32[2,512,512]{2,1,0:T(8,128)S(1)}, f32[2,8,128]{2,1,0:T(8,128)S(1)}) custom-call(s32[7]{0:T(128)S(1)} %stack.31.place_ref.refs_0_, f32[128]{0:T(128)S(1)} %copy-done.1, bf16[2,1024,512]{2,1,0:T(8,128)(2,1)S(1)} %halves.1.refs_2_, f32[256,512]{1,0:T(8,128)S(1)} %collective-permute-done.refs_3_, f32[256,512]{1,0:T(8,128)S(1)} %collective-permute-done.5.refs_4_, ...), custom_call_target="tpu_custom_call" | custom-call | flops 3221225472 | bytes 4194304 | tf_op jit(solution)/shard_map/unit/pallas_call | solution.py:46
  83.5 0.0 collective-permute-done.4.refs_4_
  83.5 4.2 %unit.7 = f32[16,264,128]{2,1,0:T(8,128)S(1)} custom-call(s32[7]{0:T(128)S(1)} %stack.31.place_ref.refs_0_, f32[128]{0:T(128)S(1)} %copy-done.1, bf16[2,1024,512]{2,1,0:T(8,128)(2,1)S(1)} %halves.1.refs_2_, f32[256,512]{1,0:T(8,128)S(1)} %collective-permute-done.1.refs_3_, f32[256,512]{1,0:T(8,128)S(1)} %collective-permute-done.4.refs_4_, ...), custom_call_target="tpu_custom_call" | custom-call | flops 3221225472 | bytes 4194304 | tf_op jit(solution)/shard_map/unit/pallas_call | solution.py:46
  87.7 35.7 %all_to_all.16.slabs_ref = f32[16,264,128]{2,1,0:T(8,128)S(1)} all-to-all(f32[16,264,128]{2,1,0:T(8,128)S(1)} %unit.7), channel_id=1, replica_groups=mesh['occ'=16,'virt'=16] {'virt'}, dimensions={0} | all-to-all | bytes 4325376 | tf_op jit(solution)/shard_map/all_to_all | solution.py:256
  123.4 0.9 finish.1
  (1 shorter events, 0.0 us)
Async XLA Ops:
  0.6 12.0 %copy-start = (s32[2,16]{1,0:T(2,128)S(1)}, s32[2,16]{1,0:T(2,128)}, u32[]{:S(2)}) copy-start(s32[2,16]{1,0:T(2,128)} %mates_ref.1) | copy-start | bytes 388
  2.5 23.8 %all-to-all-start = ((f32[16,16,512]{2,1,0:T(8,128)}), f32[16,16,512]{2,1,0:T(8,128)S(1)}, u32[]{:S(2)}, u32[]{:S(2)}) async-start(f32[16,16,512]{2,1,0:T(8,128)} %bitcast.1), calls=%async_computation | async-start | bytes 1048576 | tf_op jit(solution)/shard_map/all_to_all | solution.py:217
  16.5 0.9 copy-start.2
  26.9 37.9 %copy-start.1 = (f32[128]{0:T(128)S(1)}, f32[128]{0:T(128)}, u32[]{:S(2)}) copy-start(f32[128]{0:T(128)} %refs_1_.7) | copy-start | bytes 1540
  57.7 7.2 %collective-permute-start.3 = (f32[256,512]{1,0:T(8,128)}, f32[256,512]{1,0:T(8,128)}, u32[]{:S(2)}, u32[]{:S(2)}) collective-permute-start(f32[256,512]{1,0:T(8,128)} %get-tuple-element.23.refs_3_), channel_id=1, source_target_pairs={{0,1},{1,0},{2,3},{3,2},{4,5},{5,4},{6,7},{7,6},{8,9},{9,8},{10,11... | collective-permute-start | bytes 1572872 | tf_op jit(solution)/shard_map/ppermute | solution.py:26
  60.9 8.8 %collective-permute-start.2 = (f32[256,512]{1,0:T(8,128)S(1)}, f32[256,512]{1,0:T(8,128)}, u32[]{:S(2)}, u32[]{:S(2)}) collective-permute-start(f32[256,512]{1,0:T(8,128)S(1)} %get-tuple-element.24.refs_3_), channel_id=1, source_target_pairs={{0,1},{1,0},{2,3},{3,2},{4,5},{5,4},{6,7},{7,6},{8,9},{9,8},{10,11... | collective-permute-start | bytes 1572872 | tf_op jit(solution)/shard_map/ppermute | solution.py:26
  61.0 14.8 %collective-permute-start = (f32[256,512]{1,0:T(8,128)}, f32[256,512]{1,0:T(8,128)S(1)}, u32[]{:S(2)}, u32[]{:S(2)}) collective-permute-start(f32[256,512]{1,0:T(8,128)} %get-tuple-element.23.refs_3_), channel_id=1, source_target_pairs={{0,8},{1,9},{2,10},{3,11},{4,12},{5,13},{6,14},{7,15},{8,0},{9,1},... | collective-permute-start | bytes 1572872 | tf_op jit(solution)/shard_map/ppermute | solution.py:26
  63.6 12.7 %collective-permute-start.1 = (f32[256,512]{1,0:T(8,128)S(1)}, f32[256,512]{1,0:T(8,128)S(1)}, u32[]{:S(2)}, u32[]{:S(2)}) collective-permute-start(f32[256,512]{1,0:T(8,128)S(1)} %get-tuple-element.24.refs_3_), channel_id=1, source_target_pairs={{0,2},{1,3},{2,0},{3,1},{4,6},{5,7},{6,4},{7,5},{8,10},{9,11},{10,... | collective-permute-start | bytes 1572872 | tf_op jit(solution)/shard_map/ppermute | solution.py:26
  76.2 3.2 %collective-permute-start.5 = (f32[256,512]{1,0:T(8,128)S(1)}, f32[256,512]{1,0:T(8,128)S(1)}, u32[]{:S(2)}, u32[]{:S(2)}) collective-permute-start(f32[256,512]{1,0:T(8,128)S(1)} %collective-permute-done.refs_3_), channel_id=1, source_target_pairs={{0,1},{1,0},{2,3},{3,2},{4,5},{5,4},{6,7},{7,6},{8,9},{9,8},{10,11... | collective-permute-start | bytes 1572872 | tf_op jit(solution)/shard_map/ppermute | solution.py:26
  77.9 5.6 %collective-permute-start.4 = (f32[256,512]{1,0:T(8,128)S(1)}, f32[256,512]{1,0:T(8,128)S(1)}, u32[]{:S(2)}, u32[]{:S(2)}) collective-permute-start(f32[256,512]{1,0:T(8,128)S(1)} %collective-permute-done.1.refs_3_), channel_id=1, source_target_pairs={{0,1},{1,0},{2,3},{3,2},{4,5},{5,4},{6,7},{7,6},{8,9},{9,8},{10,11... | collective-permute-start | bytes 1572872 | tf_op jit(solution)/shard_map/ppermute | solution.py:26

commit v2 on v1

--- a/solution.py
+++ b/solution.py
@@ -16,7 +16,7 @@
 PART = PIECE // GROUPS
 SLAB = V // COLS
 ROWS = SLAB * NAUX // 128
-VMEM_LIMIT = 16 << 20
+VMEM_LIMIT = 24 << 20
 
 
 CORE, OTHERS = 1, (8, 2)
@@ -79,51 +79,72 @@
             out_refs[r][g * PART : (g + 1) * PART, :] = both_ref[g, r * PART : (r + 1) * PART, :]
 
 
-def unit_kernel(number, last, place_ref, occ_ref, own_ref, near_ref, far_ref, *rest):
+def product(own, high, low):
+    both = dot(own[...], high, 1)
+    return both[:V] + (both[V:] + dot(own[:V, :], low, 1))
+
+
+def near_kernel(own_ref, *refs):
+    mates, out_ref = refs[:ROUNDS], refs[ROUNDS]
+    for r in range(ROUNDS):
+        high, low = split(mates[r][...])
+        for n in range(2):
+            out_ref[2 * r + n] = product(own_ref.at[n], high, low)
+
+
+def unit_kernel(stage, place_ref, occ_ref, own_ref, *rest):
+    mates, rest = rest[: 2 * ROUNDS], rest[2 * ROUNDS :]
     column_ref, row_ref = rest[:2]
-    before_ref = rest[2] if number > 0 else None
-    energy_refs = rest[3:6] if last else ()
-    scratch = rest[-6:]
-    high, low = scratch[:2]
-    coulombs, amplitudes = scratch[2:4], scratch[4:]
-    grad_ref = rest[-7] if last else rest[-8]
-    for h, ref in enumerate((near_ref, far_ref)):
-        s = slice(h * HALF, (h + 1) * HALF)
+    last = stage > 0
+    if last:
+        started_ref, before_ref, early_ref, grad_ref = rest[2:6]
+    else:
+        grad_ref, energy_ref = rest[2:4]
+    high, low, coulombs, amplitudes = rest[-4:]
+    for m, ref in enumerate(mates):
+        s = slice(m * HALF, (m + 1) * HALF)
         high[s, :], low[s, :] = split(ref[...])
 
     def coulomb(n):
-        own = own_ref.at[n]
-        for b in range(2):
-            s = slice(b * HALF, (b + 1) * HALF)
-            both = dot(own[...], high[s, :], 1)
-            coulombs[n][:, s] = both[:V] + (both[V:] + dot(own[:V, :], low[s, :], 1))
+        for r in range(ROUNDS):
+            for b in range(1 if last else 0, 2):
+                s = slice((2 * r + b) * HALF, (2 * r + b + 1) * HALF)
+                coulombs[n, :, s] = product(own_ref.at[n], high[s, :], low[s, :])
+
+    def block(n, r, a, b):
+        s = slice(a * HALF, (a + 1) * HALF)
+        if last and b == 0:
+            return started_ref[2 * r + n, s, :]
+        return coulombs[n, s, (2 * r + b) * HALF : (2 * r + b + 1) * HALF]
 
     def amplitude(n):
-        shift = occ_ref[place_ref[1 + n]] + occ_ref[place_ref[3 + number]]
-        total = jnp.zeros((8, HALF), jnp.float32)
-        for a in range(2):
-            s = slice(a * HALF, (a + 1) * HALF)
-            for b in range(2):
-                t = slice(b * HALF, (b + 1) * HALF)
-                here = coulombs[n][s, t]
-                below = column_ref[s, :] + row_ref[:, t] - shift
-                value = (coulombs[n][t, s].T - 2.0 * here) / below
-                total = total + jnp.sum((value * here).reshape(HALF // 8, 8, HALF), axis=0)
-                value_high, value_low = split(value)
-                amplitudes[n][s, t] = value_high
-                amplitudes[n][V + a * HALF : V + (a + 1) * HALF, t] = value_low
-        return total[:, :128] + total[:, 128:]
+        totals = []
+        for r in range(ROUNDS):
+            shift = occ_ref[place_ref[1 + n]] + occ_ref[place_ref[3 + 2 * stage + r]]
+            total = jnp.zeros((8, HALF), jnp.float32)
+            for a in range(2):
+                s = slice(a * HALF, (a + 1) * HALF)
+                for b in range(2):
+                    here = block(n, r, a, b)
+                    below = column_ref[s, :] + row_ref[:, b * HALF : (b + 1) * HALF] - shift
+                    value = (block(n, r, b, a).T - 2.0 * here) / below
+                    total = total + jnp.sum((value * here).reshape(HALF // 8, 8, HALF), axis=0)
+                    value_high, value_low = split(value)
+                    t = slice((2 * r + b) * HALF, (2 * r + b + 1) * HALF)
+                    amplitudes[n, s, t] = value_high
+                    amplitudes[n, V + a * HALF : V + (a + 1) * HALF, t] = value_low
+            totals.append(total[:, :128] + total[:, 128:])
+        return totals
 
     def gradient(n):
         for p in range(2):
             s = slice(p * HALF, (p + 1) * HALF)
-            both = dot(amplitudes[n][...], high[:, s], 0)
-            value = both[:V] + (both[V:] + dot(amplitudes[n][:V, :], low[:, s], 0))
-            if before_ref is not None:
-                value = value + before_ref[n, :, s]
+            both = dot(amplitudes[n], high[:, s], 0)
+            value = both[:V] + (both[V:] + dot(amplitudes[n, :V, :], low[:, s], 0))
             if not last:
                 grad_ref[n, :, s] = value
                 continue
+            value = value + before_ref[n, :, s]
             for t in range(COLS):
                 to = t + place_ref[0] * (COLS // 2)
                 to = to - jnp.where(to >= COLS, COLS, 0)
@@ -142,40 +163,35 @@
         gradient(n)
     if not last:
         for n in range(2):
-            rest[-7][n] = energies[n]
+            for r in range(ROUNDS):
+                energy_ref[2 * r + n] = energies[n][r]
         return
     line = lax.broadcasted_iota(jnp.int32, (8, 128), 0)
     table = jnp.zeros((8, 128), jnp.float32)
     for n in range(2):
-        for r, value in (
-            (0, energy_refs[0][n] + energy_refs[2][n]),
-            (1, energy_refs[1][n] + energies[n]),
-        ):
-            table = jnp.where(line == 2 * r + n, jnp.sum(value, axis=0, keepdims=True), table)
+        for r in range(ROUNDS):
+            value = jnp.sum(early_ref[2 * r + n] + energies[n][r], axis=0, keepdims=True)
+            table = jnp.where(line == 2 * r + n, value, table)
     for t in range(COLS):
         grad_ref[t, 2 * ROWS :, :] = table
 
 
-def unit(number, place, occ, own, near, far, column, row, before, energies=()):
-    last = len(energies) > 0
-    args = [place, occ, own, near, far, column, row]
-    args += ([] if before is None else [before]) + list(energies)
-
+def unit(stage, *args):
     def body(*refs):
-        unit_kernel(number, last, *refs)
-
-    out = shape(COLS, 2 * ROWS + 8, 128)
+        unit_kernel(stage, *refs)
+
+    early = (shape(2, V, NAUX), shape(2 * ROUNDS, 8, 128))
     return call(
         body,
-        out if last else (shape(2, V, NAUX), shape(2, 8, 128)),
+        shape(COLS, 2 * ROWS + 8, 128) if stage else early,
         "unit",
         args,
-        scratch=[pltpu.VMEM((V, NAUX), jnp.bfloat16)] * 2
-        + [pltpu.VMEM((V, V), jnp.float32)] * 2
-        + [pltpu.VMEM((2 * V, V), jnp.bfloat16)] * 2,
+        scratch=[pltpu.VMEM((ROUNDS * V, NAUX), jnp.bfloat16)] * 2
+        + [pltpu.VMEM((2, V, ROUNDS * V), jnp.float32)]
+        + [pltpu.VMEM((2, 2 * V, ROUNDS * V), jnp.bfloat16)],
         scalars=2,
         cost=pl.CostEstimate(
-            flops=24 * V * V * NAUX, bytes_accessed=16 * V * NAUX, transcendentals=0
+            flops=48 * V * V * NAUX, bytes_accessed=16 * V * NAUX, transcendentals=0
         ),
     )
 
@@ -242,17 +258,24 @@
     both = lax.all_to_all(picked, "occ", split_axis=0, concat_axis=0, tiled=True)
     pieces = call(cut_kernel, (shape(PIECE, NAUX),) * ROUNDS, "cut", [both])
     others = [swap(piece, flip) for piece, flip in zip(pieces, OTHERS)]
-    grads, energies = None, []
-    for r in range(ROUNDS):
-        near, far = pieces[r], swap(pieces[r], CORE)
-        grads, energy = unit(r, place, occ_energy, own, near, far, column, row, grads)
-        energies.append(energy)
+    mates = []
+    for piece in pieces:
+        mates += [piece, swap(piece, CORE)]
+    grads, energy = unit(0, place, occ_energy, own, *mates, column, row)
     *others, grads = lax.optimization_barrier((*others, grads))
-    near, far = others[0], swap(others[0], CORE)
-    grads, energy = unit(2, place, occ_energy, own, near, far, column, row, grads)
-    energies.append(energy)
-    near, far = others[1], swap(others[1], CORE)
-    sent = unit(3, place, occ_energy, own, near, far, column, row, grads, energies)
+    mates = []
+    for piece in others:
+        mates += [piece, swap(piece, CORE)]
+    started = call(
+        near_kernel,
+        shape(2 * ROUNDS, V, HALF),
+        "near",
+        [own, *others],
+        cost=pl.CostEstimate(
+            flops=12 * V * V * NAUX, bytes_accessed=4 * V * NAUX, transcendentals=0
+        ),
+    )
+    sent = unit(1, place, occ_energy, own, *mates, column, row, started, grads, energy)
     slabs = lax.all_to_all(sent, "virt", split_axis=0, concat_axis=0, tiled=True)
     gradient, pair_energy = call(
         finish_kernel, (shape(OG, SLAB, NAUX), shape(ROUNDS, OG)), "finish", [slabs]

time: 125 us -> 123 us (0.984)
  Pallas kernels: 20.9 us -> 19.6 us
    pallas_call x8 -> x7, Pallas kernels: 20.9 us -> 19.6 us  [call(): pl.pallas_call(kernel, out_shape=out_shape, in_specs=[smem] * scalars + [...]
  transfers between devices with their start and end apart: 7 -> 7, of which waited for: 4 -> 4; matrix products, arithmetic and copies ran while one was open for 2% -> 2% of each run, Pallas kernels for 12% -> 9%
where the time goes in v2:
time: 123 us
  blocking collectives  65.6 us (53%)
  Pallas kernels  19.6 us (16%)
  starting transfers between devices  18.7 us (15%)
  waiting for transfers between devices  12.2 us (10%)
  local copies, waits for them, and re-layouts  4.62 us (4%)
  between operations  2.11 us (2%)
    all_to_all x1, blocking collectives, per_device(): lax.all_to_all(sent, 'virt', split_axis=0, concat_axis=0, tiled=True)  35.7 us
    all_to_all x1, blocking collectives, per_device(): lax.all_to_all(picked, 'occ', split_axis=0, concat_axis=0, tiled=True)  29.9 us
    pallas_call x7, Pallas kernels, call(): pl.pallas_call(kernel, out_shape=out_shape, in_specs=[smem] * scalars + [...  19.6 us
    all_to_all x1, starting transfers between devices, per_device(): lax.all_to_all(slab.reshape(GROUPS, PART, NAUX), 'occ', split_axis=0, con...  10 us
    all_to_all x1, waiting for transfers between devices, per_device(): lax.all_to_all(slab.reshape(GROUPS, PART, NAUX), 'occ', split_axis=0, con...  8.81 us
    ppermute x6, starting transfers between devices, swap(): return lax.ppermute(array, 'virt', [(v, v ^ flip) for v in range(COLS)])  8.7 us
    ppermute x6, waiting for transfers between devices, swap(): return lax.ppermute(array, 'virt', [(v, v ^ flip) for v in range(COLS)])  3.41 us
  transfers between devices with their start and end apart: 7, of which 4 were waited for; matrix products, arithmetic and copies ran while one was open for 2% of the time, Pallas kernels for 9%

profile of v2, /device:TPU:1, one launch (start us, length us, event | category | flops | bytes accessed | tf_op | source)
XLA Modules:
  0.0 122.9 jit_solution(1099833288282423505)
XLA Ops:
  0.6 0.0 copy-start
  0.6 0.0 copy-start.2
  0.7 1.9 %constant_dynamic-slice_fusion.2 = f32[256,512]{1,0:T(8,128)} fusion(f32[4096,512]{1,0:T(8,128)} %bitcast.16, s32[]{:T(128)S(6)} %select_n.13), kind=kLoop, calls=%fused_computation.3 | loop fusion | bytes 1048580 | tf_op jit(solution)/shard_map/dynamic_slice | solution.py:232
  2.5 10.0 %all-to-all-start = ((f32[16,16,512]{2,1,0:T(8,128)}), f32[16,16,512]{2,1,0:T(8,128)S(1)}, u32[]{:S(2)}, u32[]{:S(2)}) async-start(f32[16,16,512]{2,1,0:T(8,128)} %bitcast.1), calls=%async_computation | async-start | bytes 1048576 | tf_op jit(solution)/shard_map/all_to_all | solution.py:233
  12.6 0.0 copy-done
  12.6 0.7 constant_dynamic-slice_fusion.3
  14.6 0.0 copy-done.2
  14.6 0.1 dynamic_slice.19
  14.7 0.1 stack.31.place_ref.refs_0_
  14.8 1.8 %constant_dynamic-slice_fusion.own_ref = f32[2,512,512]{2,1,0:T(8,128)S(1)} fusion(f32[8,512,512]{2,1,0:T(8,128)} %param.4, s32[]{:T(128)S(6)} %select_n.15), kind=kLoop, calls=%fused_computation.1 | loop fusion | bytes 4194308 | tf_op jit(solution)/shard_map/dynamic_slice | solution.py:251
  16.6 0.9 halves.1.refs_2_.own_ref
  17.5 8.8 %all-to-all-done.mixed_ref = f32[16,16,512]{2,1,0:T(8,128)S(1)} async-done(((f32[16,16,512]{2,1,0:T(8,128)}), f32[16,16,512]{2,1,0:T(8,128)S(1)}, u32[]{:S(2)}, u32[]{:S(2)}) %all-to-all-start) | async-done | bytes 524320 | tf_op jit(solution)/shard_map/all_to_all | solution.py:233
  26.3 0.0 copy-start.1
  26.3 0.6 pick.1
  27.0 29.9 %all_to_all.15.both_ref = f32[16,32,512]{2,1,0:T(8,128)S(1)} all-to-all(f32[16,32,512]{2,1,0:T(8,128)S(1)} %pick.1), channel_id=1, replica_groups=mesh['occ'=16,'virt'=16] {'occ'}, dimensions={0} | all-to-all | bytes 2097152 | tf_op jit(solution)/shard_map/all_to_all | solution.py:258
  56.8 0.9 cut.1
  57.7 3.2 %collective-permute-start.2 = (f32[256,512]{1,0:T(8,128)}, f32[256,512]{1,0:T(8,128)}, u32[]{:S(2)}, u32[]{:S(2)}) collective-permute-start(f32[256,512]{1,0:T(8,128)} %get-tuple-element.19.refs_3_), channel_id=1, source_target_pairs={{0,1},{1,0},{2,3},{3,2},{4,5},{5,4},{6,7},{7,6},{8,9},{9,8},{10,11... | collective-permute-start | bytes 1572872 | tf_op jit(solution)/shard_map/ppermute | solution.py:26
  60.9 0.0 collective-permute-start.3
  60.9 0.1 copy.6.refs_7_
  61.0 2.5 %collective-permute-start = (f32[256,512]{1,0:T(8,128)}, f32[256,512]{1,0:T(8,128)S(1)}, u32[]{:S(2)}, u32[]{:S(2)}) collective-permute-start(f32[256,512]{1,0:T(8,128)} %get-tuple-element.19.refs_3_), channel_id=1, source_target_pairs={{0,8},{1,9},{2,10},{3,11},{4,12},{5,13},{6,14},{7,15},{8,0},{9,1},... | collective-permute-start | bytes 1572872 | tf_op jit(solution)/shard_map/ppermute | solution.py:26
  63.6 1.3 %collective-permute-start.1 = (f32[256,512]{1,0:T(8,128)S(1)}, f32[256,512]{1,0:T(8,128)S(1)}, u32[]{:S(2)}, u32[]{:S(2)}) collective-permute-start(f32[256,512]{1,0:T(8,128)S(1)} %get-tuple-element.20.refs_5_), channel_id=1, source_target_pairs={{0,2},{1,3},{2,0},{3,1},{4,6},{5,7},{6,4},{7,5},{8,10},{9,11},{10,... | collective-permute-start | bytes 1572872 | tf_op jit(solution)/shard_map/ppermute | solution.py:26
  64.9 0.0 collective-permute-done.2.refs_4_
  64.9 0.0 collective-permute-done.3.refs_6_
  64.9 0.0 copy-done.1
  64.9 8.4 %unit.2 = (f32[2,512,512]{2,1,0:T(8,128)S(1)}, f32[4,8,128]{2,1,0:T(8,128)S(1)}) custom-call(s32[7]{0:T(128)S(1)} %stack.31.place_ref.refs_0_, f32[128]{0:T(128)S(1)} %copy-done.1, bf16[2,1024,512]{2,1,0:T(8,128)(2,1)S(1)} %halves.1.refs_2_.own_ref, f32[256,512]{1,0:T(8,128)} %get-tuple-element.19.refs_3_, f32[256,512]{1,0:T(8,128)} %collective-permute-done.2.refs_4_, ...), custom_call_target="tpu_custom_call" | custom-call | flops 6442450944 | bytes 4194304 | tf_op jit(solution)/shard_map/unit/pallas_call | solution.py:46
  73.3 2.5 %collective-permute-done.refs_0_.refs_3_ = f32[256,512]{1,0:T(8,128)S(1)} collective-permute-done((f32[256,512]{1,0:T(8,128)}, f32[256,512]{1,0:T(8,128)S(1)}, u32[]{:S(2)}, u32[]{:S(2)}) %collective-permute-start) | collective-permute-done | bytes 524320 | tf_op jit(solution)/shard_map/ppermute | solution.py:26
  75.8 0.4 collective-permute-done.1.refs_1_.refs_5_
  76.2 1.7 %collective-permute-start.4 = (f32[256,512]{1,0:T(8,128)S(1)}, f32[256,512]{1,0:T(8,128)S(1)}, u32[]{:S(2)}, u32[]{:S(2)}) collective-permute-start(f32[256,512]{1,0:T(8,128)S(1)} %collective-permute-done.refs_0_.refs_3_), channel_id=1, source_target_pairs={{0,1},{1,0},{2,3},{3,2},{4,5},{5,4},{6,7},{7,6},{8,9},{9,8},{10,11... | collective-permute-start | bytes 1572872 | tf_op jit(solution)/shard_map/ppermute | solution.py:26
  77.9 0.0 collective-permute-start.5
  77.9 1.8 %near.1.refs_9_ = f32[4,512,256]{2,1,0:T(8,128)S(1)} custom-call(bf16[2,1024,512]{2,1,0:T(8,128)(2,1)S(1)} %halves.1.refs_2_.own_ref, f32[256,512]{1,0:T(8,128)S(1)} %collective-permute-done.refs_0_.refs_3_, f32[256,512]{1,0:T(8,128)S(1)} %collective-permute-done.1.refs_1_.refs_5_), custom_call_target="tpu_custom_call" | custom-call | flops 1610612736 | bytes 1048576 | tf_op jit(solution)/shard_map/near/pallas_call | solution.py:46
  79.7 0.0 collective-permute-done.4.refs_4_
  79.7 0.5 collective-permute-done.5.refs_6_
  80.2 6.1 %unit.3 = f32[16,264,128]{2,1,0:T(8,128)S(1)} custom-call(s32[7]{0:T(128)S(1)} %stack.31.place_ref.refs_0_, f32[128]{0:T(128)S(1)} %copy-done.1, bf16[2,1024,512]{2,1,0:T(8,128)(2,1)S(1)} %halves.1.refs_2_.own_ref, f32[256,512]{1,0:T(8,128)S(1)} %collective-permute-done.refs_0_.refs_3_, f32[256,512]{1,0:T(8,128)S(1)} %collective-permute-done.4.refs_4_, ...), custom_call_target="tpu_custom_call" | custom-call | flops 6442450944 | bytes 4194304 | tf_op jit(solution)/shard_map/unit/pallas_call | solution.py:46
  86.3 35.7 %all_to_all.16.slabs_ref = f32[16,264,128]{2,1,0:T(8,128)S(1)} all-to-all(f32[16,264,128]{2,1,0:T(8,128)S(1)} %unit.3), channel_id=1, replica_groups=mesh['occ'=16,'virt'=16] {'virt'}, dimensions={0} | all-to-all | bytes 4325376 | tf_op jit(solution)/shard_map/all_to_all | solution.py:279
  122.0 0.9 finish.1
  (1 shorter events, 0.0 us)
Async XLA Ops:
  0.6 12.0 %copy-start = (s32[2,16]{1,0:T(2,128)S(1)}, s32[2,16]{1,0:T(2,128)}, u32[]{:S(2)}) copy-start(s32[2,16]{1,0:T(2,128)} %mates_ref.1) | copy-start | bytes 388
  0.6 14.0 %copy-start.2 = (f32[512]{0:T(512)S(1)}, f32[512]{0:T(512)}, u32[]{:S(2)}) copy-start(f32[512]{0:T(512)} %param.6) | copy-start | bytes 6148
  2.5 23.8 %all-to-all-start = ((f32[16,16,512]{2,1,0:T(8,128)}), f32[16,16,512]{2,1,0:T(8,128)S(1)}, u32[]{:S(2)}, u32[]{:S(2)}) async-start(f32[16,16,512]{2,1,0:T(8,128)} %bitcast.1), calls=%async_computation | async-start | bytes 1048576 | tf_op jit(solution)/shard_map/all_to_all | solution.py:233
  26.3 38.5 %copy-start.1 = (f32[128]{0:T(128)S(1)}, f32[128]{0:T(128)}, u32[]{:S(2)}) copy-start(f32[128]{0:T(128)} %refs_1_.3) | copy-start | bytes 1540
  57.7 7.2 %collective-permute-start.2 = (f32[256,512]{1,0:T(8,128)}, f32[256,512]{1,0:T(8,128)}, u32[]{:S(2)}, u32[]{:S(2)}) collective-permute-start(f32[256,512]{1,0:T(8,128)} %get-tuple-element.19.refs_3_), channel_id=1, source_target_pairs={{0,1},{1,0},{2,3},{3,2},{4,5},{5,4},{6,7},{7,6},{8,9},{9,8},{10,11... | collective-permute-start | bytes 1572872 | tf_op jit(solution)/shard_map/ppermute | solution.py:26
  60.9 4.0 %collective-permute-start.3 = (f32[256,512]{1,0:T(8,128)S(1)}, f32[256,512]{1,0:T(8,128)}, u32[]{:S(2)}, u32[]{:S(2)}) collective-permute-start(f32[256,512]{1,0:T(8,128)S(1)} %get-tuple-element.20.refs_5_), channel_id=1, source_target_pairs={{0,1},{1,0},{2,3},{3,2},{4,5},{5,4},{6,7},{7,6},{8,9},{9,8},{10,11... | collective-permute-start | bytes 1572872 | tf_op jit(solution)/shard_map/ppermute | solution.py:26
  61.0 14.8 %collective-permute-start = (f32[256,512]{1,0:T(8,128)}, f32[256,512]{1,0:T(8,128)S(1)}, u32[]{:S(2)}, u32[]{:S(2)}) collective-permute-start(f32[256,512]{1,0:T(8,128)} %get-tuple-element.19.refs_3_), channel_id=1, source_target_pairs={{0,8},{1,9},{2,10},{3,11},{4,12},{5,13},{6,14},{7,15},{8,0},{9,1},... | collective-permute-start | bytes 1572872 | tf_op jit(solution)/shard_map/ppermute | solution.py:26
  63.6 12.7 %collective-permute-start.1 = (f32[256,512]{1,0:T(8,128)S(1)}, f32[256,512]{1,0:T(8,128)S(1)}, u32[]{:S(2)}, u32[]{:S(2)}) collective-permute-start(f32[256,512]{1,0:T(8,128)S(1)} %get-tuple-element.20.refs_5_), channel_id=1, source_target_pairs={{0,2},{1,3},{2,0},{3,1},{4,6},{5,7},{6,4},{7,5},{8,10},{9,11},{10,... | collective-permute-start | bytes 1572872 | tf_op jit(solution)/shard_map/ppermute | solution.py:26
  76.2 3.5 %collective-permute-start.4 = (f32[256,512]{1,0:T(8,128)S(1)}, f32[256,512]{1,0:T(8,128)S(1)}, u32[]{:S(2)}, u32[]{:S(2)}) collective-permute-start(f32[256,512]{1,0:T(8,128)S(1)} %collective-permute-done.refs_0_.refs_3_), channel_id=1, source_target_pairs={{0,1},{1,0},{2,3},{3,2},{4,5},{5,4},{6,7},{7,6},{8,9},{9,8},{10,11... | collective-permute-start | bytes 1572872 | tf_op jit(solution)/shard_map/ppermute | solution.py:26
  77.9 2.3 %collective-permute-start.5 = (f32[256,512]{1,0:T(8,128)S(1)}, f32[256,512]{1,0:T(8,128)S(1)}, u32[]{:S(2)}, u32[]{:S(2)}) collective-permute-start(f32[256,512]{1,0:T(8,128)S(1)} %collective-permute-done.1.refs_1_.refs_5_), channel_id=1, source_target_pairs={{0,1},{1,0},{2,3},{3,2},{4,5},{5,4},{6,7},{7,6},{8,9},{9,8},{10,11... | collective-permute-start | bytes 1572872 | tf_op jit(solution)/shard_map/ppermute | solution.py:26

commit v3 on v2

--- a/solution.py
+++ b/solution.py
@@ -19,7 +19,7 @@
 VMEM_LIMIT = 24 << 20
 
 
-CORE, OTHERS = 1, (8, 2)
+CORE, OTHERS = 1, (2, 6)
 
 
 def swap(array, flip):
@@ -197,30 +197,52 @@
 
 
 def finish_kernel(slabs_ref, grad_ref, energy_ref):
+    step = pl.program_id(0)
+    quad, core = step // 2, step % 2
     line = lax.broadcasted_iota(jnp.int32, (8, 128), 0)
     lane = lax.broadcasted_iota(jnp.int32, (8, 128), 1)
     table = jnp.zeros((8, 128), jnp.float32)
-
-    def added(sources, rows):
+    sources = [x * 8 + y * 4 + quad * 2 + core for x in range(2) for y in range(2)]
+
+    def added(rows):
         values = [slabs_ref[s, rows, :] for s in sources]
         return (values[0] + values[1]) + (values[2] + values[3])
 
-    for quad in range(2):
-        for core in range(2):
-            sources = [(quad ^ (y & 1)) * 8 + y * 2 + core for y in range(4)]
-            energy = jnp.sum(added(sources, slice(2 * ROWS, 2 * ROWS + 8)), axis=1, keepdims=True)
-            for n in range(2):
-                i = quad * 4 + core * 2 + n
-                for p in range(4):
-                    for q in range(4):
-                        at_row = n * ROWS + (4 * p + q) * 8
-                        grad_ref[i, 8 * p : 8 * p + 8, q * 128 : (q + 1) * 128] = added(
-                            sources, slice(at_row, at_row + 8)
-                        )
-                for r in range(ROUNDS):
-                    value = energy[2 * r + n : 2 * r + n + 1]
-                    table = jnp.where((line == r) & (lane == i), value, table)
-    energy_ref[...] = table[:ROUNDS, :OG] * (1.0 / (V * OG * V))
+    energy = jnp.sum(added(slice(2 * ROWS, 2 * ROWS + 8)), axis=1, keepdims=True)
+    for n in range(2):
+        for p in range(4):
+            for q in range(4):
+                at_row = n * ROWS + (4 * p + q) * 8
+                grad_ref[n, 8 * p : 8 * p + 8, q * 128 : (q + 1) * 128] = added(
+                    slice(at_row, at_row + 8)
+                )
+        for r in range(ROUNDS):
+            value = energy[2 * r + n : 2 * r + n + 1]
+            table = jnp.where((line == r) & (lane == 2 * step + n), value, table)
+    table = table[:ROUNDS, :OG] * (1.0 / (V * OG * V))
+
+    @pl.when(step == 0)
+    def _():
+        energy_ref[...] = table
+
+    @pl.when(step > 0)
+    def _():
+        energy_ref[...] = energy_ref[...] + table
+
+
+def finish(slabs):
+    return pl.pallas_call(
+        finish_kernel,
+        out_shape=(shape(OG, SLAB, NAUX), shape(ROUNDS, OG)),
+        grid=(OG // 2,),
+        in_specs=[pl.BlockSpec(memory_space=pltpu.VMEM)],
+        out_specs=(
+            pl.BlockSpec((2, SLAB, NAUX), lambda p: (p, 0, 0)),
+            pl.BlockSpec((ROUNDS, OG), lambda p: (0, 0)),
+        ),
+        compiler_params=pltpu.CompilerParams(vmem_limit_bytes=VMEM_LIMIT),
+        name="finish",
+    )(slabs)
 
 
 def per_device(factors, occ_energy, virt_energy, pairing):
@@ -233,12 +255,12 @@
     mixed = lax.all_to_all(
         slab.reshape(GROUPS, PART, NAUX), "occ", split_axis=0, concat_axis=0, tiled=True
     )
-    orbital = (x ^ (y & 1)) * 4 + core * 2
+    orbital = (y & 1) * 4 + core * 2
     mates = [pairing[r, group] * OG for r in range(ROUNDS)]
     j = x * 4 + y
     place = jnp.stack(
         [core, group * OG + orbital, group * OG + orbital + 1]
-        + [mates[0] + j, mates[1] + j, mates[0] + (j ^ 4), mates[1] + (j ^ 1)]
+        + [mates[0] + j, mates[1] + j, mates[0] + (j ^ 1), mates[1] + (j ^ 3)]
     ).astype(jnp.int32)
     turned = lax.dynamic_slice_in_dim(
         jnp.concatenate([virt_energy, virt_energy]), core * HALF, V, 0
@@ -277,9 +299,7 @@
     )
     sent = unit(1, place, occ_energy, own, *mates, column, row, started, grads, energy)
     slabs = lax.all_to_all(sent, "virt", split_axis=0, concat_axis=0, tiled=True)
-    gradient, pair_energy = call(
-        finish_kernel, (shape(OG, SLAB, NAUX), shape(ROUNDS, OG)), "finish", [slabs]
-    )
+    gradient, pair_energy = finish(slabs)
     return (pair_energy, gradient)
 
 

time: 123 us -> 124 us (level)
    pallas_call x0 -> x1, Pallas kernels: none -> 1.58 us  [finish(): pl.pallas_call(finish_kernel, out_shape=(shape(OG, SLAB, NAUX), shape(ROU...]
    pallas_call x7 -> x6, Pallas kernels: 19.6 us -> 18.7 us  [call(): pl.pallas_call(kernel, out_shape=out_shape, in_specs=[smem] * scalars + [...]
where the time goes in v3:
time: 124 us; the launch traced here: 123 us
  blocking collectives  65.3 us (53%)
  Pallas kernels  20.3 us (16%)
  starting transfers between devices  18.2 us (15%)
  waiting for transfers between devices  12.8 us (10%)
  local copies, waits for them, and re-layouts  4.62 us (4%)
  between operations  2.1 us (2%)
    all_to_all x1, blocking collectives, per_device(): lax.all_to_all(sent, 'virt', split_axis=0, concat_axis=0, tiled=True)  35.4 us
    all_to_all x1, blocking collectives, per_device(): lax.all_to_all(picked, 'occ', split_axis=0, concat_axis=0, tiled=True)  29.9 us
    pallas_call x6, Pallas kernels, call(): pl.pallas_call(kernel, out_shape=out_shape, in_specs=[smem] * scalars + [...  18.7 us
    all_to_all x1, starting transfers between devices, per_device(): lax.all_to_all(slab.reshape(GROUPS, PART, NAUX), 'occ', split_axis=0, con...  10 us
    all_to_all x1, waiting for transfers between devices, per_device(): lax.all_to_all(slab.reshape(GROUPS, PART, NAUX), 'occ', split_axis=0, con...  8.82 us
    ppermute x6, starting transfers between devices, swap(): return lax.ppermute(array, 'virt', [(v, v ^ flip) for v in range(COLS)])  8.15 us
    ppermute x6, waiting for transfers between devices, swap(): return lax.ppermute(array, 'virt', [(v, v ^ flip) for v in range(COLS)])  4.01 us
  transfers between devices with their start and end apart: 7, of which 4 were waited for; matrix products, arithmetic and copies ran while one was open for 2% of the time, Pallas kernels for 9%

profile of v3, /device:TPU:1, one launch (start us, length us, event | category | flops | bytes accessed | tf_op | source)
XLA Modules:
  0.0 123.4 jit_solution(531665805884331860)
XLA Ops:
  0.6 0.0 copy-start
  0.6 0.0 copy-start.2
  0.7 1.9 %constant_dynamic-slice_fusion.2 = f32[256,512]{1,0:T(8,128)} fusion(f32[4096,512]{1,0:T(8,128)} %bitcast.16, s32[]{:T(128)S(6)} %select_n.13), kind=kLoop, calls=%fused_computation.3 | loop fusion | bytes 1048580 | tf_op jit(solution)/shard_map/dynamic_slice | solution.py:254
  2.5 10.0 %all-to-all-start = ((f32[16,16,512]{2,1,0:T(8,128)}), f32[16,16,512]{2,1,0:T(8,128)S(1)}, u32[]{:S(2)}, u32[]{:S(2)}) async-start(f32[16,16,512]{2,1,0:T(8,128)} %bitcast.1), calls=%async_computation | async-start | bytes 1048576 | tf_op jit(solution)/shard_map/all_to_all | solution.py:255
  12.6 0.0 copy-done
  12.6 0.7 constant_dynamic-slice_fusion.3
  14.6 0.0 copy-done.2
  14.6 0.1 dynamic_slice.19
  14.7 0.1 stack.31.place_ref.refs_0_
  14.8 1.8 %constant_dynamic-slice_fusion.own_ref = f32[2,512,512]{2,1,0:T(8,128)S(1)} fusion(f32[8,512,512]{2,1,0:T(8,128)} %param.4, s32[]{:T(128)S(6)} %select_n.15), kind=kLoop, calls=%fused_computation.1 | loop fusion | bytes 4194308 | tf_op jit(solution)/shard_map/dynamic_slice | solution.py:273
  16.6 0.9 halves.1.refs_2_.own_ref
  17.5 8.8 %all-to-all-done.mixed_ref = f32[16,16,512]{2,1,0:T(8,128)S(1)} async-done(((f32[16,16,512]{2,1,0:T(8,128)}), f32[16,16,512]{2,1,0:T(8,128)S(1)}, u32[]{:S(2)}, u32[]{:S(2)}) %all-to-all-start) | async-done | bytes 524320 | tf_op jit(solution)/shard_map/all_to_all | solution.py:255
  26.3 0.0 copy-start.1
  26.3 0.6 pick.1
  27.0 29.9 %all_to_all.15.both_ref = f32[16,32,512]{2,1,0:T(8,128)S(1)} all-to-all(f32[16,32,512]{2,1,0:T(8,128)S(1)} %pick.1), channel_id=1, replica_groups=mesh['occ'=16,'virt'=16] {'occ'}, dimensions={0} | all-to-all | bytes 2097152 | tf_op jit(solution)/shard_map/all_to_all | solution.py:280
  56.8 0.9 cut.1
  57.7 3.2 %collective-permute-start.2 = (f32[256,512]{1,0:T(8,128)}, f32[256,512]{1,0:T(8,128)}, u32[]{:S(2)}, u32[]{:S(2)}) collective-permute-start(f32[256,512]{1,0:T(8,128)} %get-tuple-element.19.refs_3_), channel_id=1, source_target_pairs={{0,1},{1,0},{2,3},{3,2},{4,5},{5,4},{6,7},{7,6},{8,9},{9,8},{10,11... | collective-permute-start | bytes 1572872 | tf_op jit(solution)/shard_map/ppermute | solution.py:26
  60.9 0.0 collective-permute-start.3
  60.9 0.1 copy.6.refs_7_
  61.0 1.4 %collective-permute-start = (f32[256,512]{1,0:T(8,128)}, f32[256,512]{1,0:T(8,128)S(1)}, u32[]{:S(2)}, u32[]{:S(2)}) collective-permute-start(f32[256,512]{1,0:T(8,128)} %get-tuple-element.19.refs_3_), channel_id=1, source_target_pairs={{0,2},{1,3},{2,0},{3,1},{4,6},{5,7},{6,4},{7,5},{8,10},{9,11},{10,... | collective-permute-start | bytes 1572872 | tf_op jit(solution)/shard_map/ppermute | solution.py:26
  62.4 1.9 %collective-permute-start.1 = (f32[256,512]{1,0:T(8,128)S(1)}, f32[256,512]{1,0:T(8,128)S(1)}, u32[]{:S(2)}, u32[]{:S(2)}) collective-permute-start(f32[256,512]{1,0:T(8,128)S(1)} %get-tuple-element.20.refs_5_), channel_id=1, source_target_pairs={{0,6},{1,7},{2,4},{3,5},{4,2},{5,3},{6,0},{7,1},{8,14},{9,15},{10,... | collective-permute-start | bytes 1572872 | tf_op jit(solution)/shard_map/ppermute | solution.py:26
  64.3 0.0 collective-permute-done.2.refs_4_
  64.3 0.0 collective-permute-done.3.refs_6_
  64.3 0.0 copy-done.1
  64.3 8.4 %unit.2 = (f32[2,512,512]{2,1,0:T(8,128)S(1)}, f32[4,8,128]{2,1,0:T(8,128)S(1)}) custom-call(s32[7]{0:T(128)S(1)} %stack.31.place_ref.refs_0_, f32[128]{0:T(128)S(1)} %copy-done.1, bf16[2,1024,512]{2,1,0:T(8,128)(2,1)S(1)} %halves.1.refs_2_.own_ref, f32[256,512]{1,0:T(8,128)} %get-tuple-element.19.refs_3_, f32[256,512]{1,0:T(8,128)} %collective-permute-done.2.refs_4_, ...), custom_call_target="tpu_custom_call" | custom-call | flops 6442450944 | bytes 4194304 | tf_op jit(solution)/shard_map/unit/pallas_call | solution.py:46
  72.7 1.6 %collective-permute-done.refs_0_.refs_3_ = f32[256,512]{1,0:T(8,128)S(1)} collective-permute-done((f32[256,512]{1,0:T(8,128)}, f32[256,512]{1,0:T(8,128)S(1)}, u32[]{:S(2)}, u32[]{:S(2)}) %collective-permute-start) | collective-permute-done | bytes 524320 | tf_op jit(solution)/shard_map/ppermute | solution.py:26
  74.3 2.0 %collective-permute-done.1.refs_1_.refs_5_ = f32[256,512]{1,0:T(8,128)S(1)} collective-permute-done((f32[256,512]{1,0:T(8,128)S(1)}, f32[256,512]{1,0:T(8,128)S(1)}, u32[]{:S(2)}, u32[]{:S(2)}) %collective-permute-start.1) | collective-permute-done | bytes 524320 | tf_op jit(solution)/shard_map/ppermute | solution.py:26
  76.3 1.7 %collective-permute-start.4 = (f32[256,512]{1,0:T(8,128)S(1)}, f32[256,512]{1,0:T(8,128)S(1)}, u32[]{:S(2)}, u32[]{:S(2)}) collective-permute-start(f32[256,512]{1,0:T(8,128)S(1)} %collective-permute-done.refs_0_.refs_3_), channel_id=1, source_target_pairs={{0,1},{1,0},{2,3},{3,2},{4,5},{5,4},{6,7},{7,6},{8,9},{9,8},{10,11... | collective-permute-start | bytes 1572872 | tf_op jit(solution)/shard_map/ppermute | solution.py:26
  78.0 0.0 collective-permute-start.5
  78.0 1.8 %near.1.refs_9_ = f32[4,512,256]{2,1,0:T(8,128)S(1)} custom-call(bf16[2,1024,512]{2,1,0:T(8,128)(2,1)S(1)} %halves.1.refs_2_.own_ref, f32[256,512]{1,0:T(8,128)S(1)} %collective-permute-done.refs_0_.refs_3_, f32[256,512]{1,0:T(8,128)S(1)} %collective-permute-done.1.refs_1_.refs_5_), custom_call_target="tpu_custom_call" | custom-call | flops 1610612736 | bytes 1048576 | tf_op jit(solution)/shard_map/near/pallas_call | solution.py:46
  79.8 0.0 collective-permute-done.4.refs_4_
  79.8 0.4 collective-permute-done.5.refs_6_
  80.2 6.1 %unit.3 = f32[16,264,128]{2,1,0:T(8,128)S(1)} custom-call(s32[7]{0:T(128)S(1)} %stack.31.place_ref.refs_0_, f32[128]{0:T(128)S(1)} %copy-done.1, bf16[2,1024,512]{2,1,0:T(8,128)(2,1)S(1)} %halves.1.refs_2_.own_ref, f32[256,512]{1,0:T(8,128)S(1)} %collective-permute-done.refs_0_.refs_3_, f32[256,512]{1,0:T(8,128)S(1)} %collective-permute-done.4.refs_4_, ...), custom_call_target="tpu_custom_call" | custom-call | flops 6442450944 | bytes 4194304 | tf_op jit(solution)/shard_map/unit/pallas_call | solution.py:46
  86.4 35.4 %all_to_all.16.slabs_ref = f32[16,264,128]{2,1,0:T(8,128)S(1)} all-to-all(f32[16,264,128]{2,1,0:T(8,128)S(1)} %unit.3), channel_id=1, replica_groups=mesh['occ'=16,'virt'=16] {'virt'}, dimensions={0} | all-to-all | bytes 4325376 | tf_op jit(solution)/shard_map/all_to_all | solution.py:301
  121.8 1.6 %finish.1 = (f32[8,32,512]{2,1,0:T(8,128)}, f32[2,8]{1,0:T(2,128)}) custom-call(f32[16,264,128]{2,1,0:T(8,128)S(1)} %all_to_all.16.slabs_ref), custom_call_target="tpu_custom_call" | custom-call | tf_op jit(solution)/shard_map/finish/pallas_call | solution.py:234
  (1 shorter events, 0.0 us)
Async XLA Ops:
  0.6 12.0 %copy-start = (s32[2,16]{1,0:T(2,128)S(1)}, s32[2,16]{1,0:T(2,128)}, u32[]{:S(2)}) copy-start(s32[2,16]{1,0:T(2,128)} %mates_ref.1) | copy-start | bytes 388
  0.6 14.0 %copy-start.2 = (f32[512]{0:T(512)S(1)}, f32[512]{0:T(512)}, u32[]{:S(2)}) copy-start(f32[512]{0:T(512)} %param.6) | copy-start | bytes 6148
  2.5 23.8 %all-to-all-start = ((f32[16,16,512]{2,1,0:T(8,128)}), f32[16,16,512]{2,1,0:T(8,128)S(1)}, u32[]{:S(2)}, u32[]{:S(2)}) async-start(f32[16,16,512]{2,1,0:T(8,128)} %bitcast.1), calls=%async_computation | async-start | bytes 1048576 | tf_op jit(solution)/shard_map/all_to_all | solution.py:255
  26.3 38.0 %copy-start.1 = (f32[128]{0:T(128)S(1)}, f32[128]{0:T(128)}, u32[]{:S(2)}) copy-start(f32[128]{0:T(128)} %refs_1_.3) | copy-start | bytes 1540
  57.7 6.6 %collective-permute-start.2 = (f32[256,512]{1,0:T(8,128)}, f32[256,512]{1,0:T(8,128)}, u32[]{:S(2)}, u32[]{:S(2)}) collective-permute-start(f32[256,512]{1,0:T(8,128)} %get-tuple-element.19.refs_3_), channel_id=1, source_target_pairs={{0,1},{1,0},{2,3},{3,2},{4,5},{5,4},{6,7},{7,6},{8,9},{9,8},{10,11... | collective-permute-start | bytes 1572872 | tf_op jit(solution)/shard_map/ppermute | solution.py:26
  60.9 3.4 %collective-permute-start.3 = (f32[256,512]{1,0:T(8,128)S(1)}, f32[256,512]{1,0:T(8,128)}, u32[]{:S(2)}, u32[]{:S(2)}) collective-permute-start(f32[256,512]{1,0:T(8,128)S(1)} %get-tuple-element.20.refs_5_), channel_id=1, source_target_pairs={{0,1},{1,0},{2,3},{3,2},{4,5},{5,4},{6,7},{7,6},{8,9},{9,8},{10,11... | collective-permute-start | bytes 1572872 | tf_op jit(solution)/shard_map/ppermute | solution.py:26
  61.0 13.3 %collective-permute-start = (f32[256,512]{1,0:T(8,128)}, f32[256,512]{1,0:T(8,128)S(1)}, u32[]{:S(2)}, u32[]{:S(2)}) collective-permute-start(f32[256,512]{1,0:T(8,128)} %get-tuple-element.19.refs_3_), channel_id=1, source_target_pairs={{0,2},{1,3},{2,0},{3,1},{4,6},{5,7},{6,4},{7,5},{8,10},{9,11},{10,... | collective-permute-start | bytes 1572872 | tf_op jit(solution)/shard_map/ppermute | solution.py:26
  62.4 13.9 %collective-permute-start.1 = (f32[256,512]{1,0:T(8,128)S(1)}, f32[256,512]{1,0:T(8,128)S(1)}, u32[]{:S(2)}, u32[]{:S(2)}) collective-permute-start(f32[256,512]{1,0:T(8,128)S(1)} %get-tuple-element.20.refs_5_), channel_id=1, source_target_pairs={{0,6},{1,7},{2,4},{3,5},{4,2},{5,3},{6,0},{7,1},{8,14},{9,15},{10,... | collective-permute-start | bytes 1572872 | tf_op jit(solution)/shard_map/ppermute | solution.py:26
  76.3 3.5 %collective-permute-start.4 = (f32[256,512]{1,0:T(8,128)S(1)}, f32[256,512]{1,0:T(8,128)S(1)}, u32[]{:S(2)}, u32[]{:S(2)}) collective-permute-start(f32[256,512]{1,0:T(8,128)S(1)} %collective-permute-done.refs_0_.refs_3_), channel_id=1, source_target_pairs={{0,1},{1,0},{2,3},{3,2},{4,5},{5,4},{6,7},{7,6},{8,9},{9,8},{10,11... | collective-permute-start | bytes 1572872 | tf_op jit(solution)/shard_map/ppermute | solution.py:26
  78.0 2.3 %collective-permute-start.5 = (f32[256,512]{1,0:T(8,128)S(1)}, f32[256,512]{1,0:T(8,128)S(1)}, u32[]{:S(2)}, u32[]{:S(2)}) collective-permute-start(f32[256,512]{1,0:T(8,128)S(1)} %collective-permute-done.1.refs_1_.refs_5_), channel_id=1, source_target_pairs={{0,1},{1,0},{2,3},{3,2},{4,5},{5,4},{6,7},{7,6},{8,9},{9,8},{10,11... | collective-permute-start | bytes 1572872 | tf_op jit(solution)/shard_map/ppermute | solution.py:26

commit v4 on v3

--- a/solution.py
+++ b/solution.py
@@ -76,7 +76,9 @@
 def cut_kernel(both_ref, *out_refs):
     for g in range(GROUPS):
         for r in range(ROUNDS):
-            out_refs[r][g * PART : (g + 1) * PART, :] = both_ref[g, r * PART : (r + 1) * PART, :]
+            rows = both_ref[g, r * PART : (r + 1) * PART, :]
+            out_refs[r][g * PART : (g + 1) * PART, :] = rows
+            out_refs[ROUNDS][r, g * PART : (g + 1) * PART, :] = rows
 
 
 def product(own, high, low):
@@ -103,7 +105,7 @@
     high, low, coulombs, amplitudes = rest[-4:]
     for m, ref in enumerate(mates):
         s = slice(m * HALF, (m + 1) * HALF)
-        high[s, :], low[s, :] = split(ref[...])
+        high[s, :], low[s, :] = split(ref[...] if len(ref.shape) == 2 else ref[m // 2])
 
     def coulomb(n):
         for r in range(ROUNDS):
@@ -278,11 +280,13 @@
         pick_kernel, shape(GROUPS, ROUNDS * PART, NAUX), "pick", [pairing, mixed], scalars=1
     )
     both = lax.all_to_all(picked, "occ", split_axis=0, concat_axis=0, tiled=True)
-    pieces = call(cut_kernel, (shape(PIECE, NAUX),) * ROUNDS, "cut", [both])
+    *pieces, together = call(
+        cut_kernel, (shape(PIECE, NAUX),) * ROUNDS + (shape(ROUNDS, PIECE, NAUX),), "cut", [both]
+    )
     others = [swap(piece, flip) for piece, flip in zip(pieces, OTHERS)]
-    mates = []
+    mates, swapped = [], swap(together, CORE)
     for piece in pieces:
-        mates += [piece, swap(piece, CORE)]
+        mates += [piece, swapped]
     grads, energy = unit(0, place, occ_energy, own, *mates, column, row)
     *others, grads = lax.optimization_barrier((*others, grads))
     mates = []

time: 124 us -> 125 us (level)
  local copies, waits for them, and re-layouts: 4.62 us -> 6.46 us
    unnamed x6 -> x10, local copies, waits for them, and re-layouts: 0.01 us -> 1.85 us
    ppermute x6 -> x5, waiting for transfers between devices: 4.01 us -> 3.31 us  [swap(): return lax.ppermute(array, 'virt', [(v, v ^ flip) for v in range(COLS)])]
    ppermute x6 -> x5, starting transfers between devices: 8.15 us -> 7.57 us  [swap(): return lax.ppermute(array, 'virt', [(v, v ^ flip) for v in range(COLS)])]
  transfers between devices with their start and end apart: 7 -> 6, of which waited for: 4 -> 4; matrix products, arithmetic and copies ran while one was open for 2% -> 2% of each run, Pallas kernels for 9% -> 9%
where the time goes in v4:
time: 125 us; the launch traced here: 124 us
  blocking collectives  65.3 us (52%)
  Pallas kernels  20.8 us (17%)
  starting transfers between devices  17.6 us (14%)
  waiting for transfers between devices  12.2 us (10%)
  local copies, waits for them, and re-layouts  6.46 us (5%)
  between operations  2.01 us (2%)
    all_to_all x1, blocking collectives, per_device(): lax.all_to_all(sent, 'virt', split_axis=0, concat_axis=0, tiled=True)  35.4 us
    all_to_all x1, blocking collectives, per_device(): lax.all_to_all(picked, 'occ', split_axis=0, concat_axis=0, tiled=True)  29.9 us
    pallas_call x6, Pallas kernels, call(): pl.pallas_call(kernel, out_shape=out_shape, in_specs=[smem] * scalars + [...  19.2 us
    all_to_all x1, starting transfers between devices, per_device(): lax.all_to_all(slab.reshape(GROUPS, PART, NAUX), 'occ', split_axis=0, con...  10 us
    all_to_all x1, waiting for transfers between devices, per_device(): lax.all_to_all(slab.reshape(GROUPS, PART, NAUX), 'occ', split_axis=0, con...  8.91 us
    ppermute x5, starting transfers between devices, swap(): return lax.ppermute(array, 'virt', [(v, v ^ flip) for v in range(COLS)])  7.57 us
    ppermute x5, waiting for transfers between devices, swap(): return lax.ppermute(array, 'virt', [(v, v ^ flip) for v in range(COLS)])  3.31 us
  transfers between devices with their start and end apart: 6, of which 4 were waited for; matrix products, arithmetic and copies ran while one was open for 2% of the time, Pallas kernels for 9%

profile of v4, /device:TPU:1, one launch (start us, length us, event | category | flops | bytes accessed | tf_op | source)
XLA Modules:
  0.0 124.4 jit_solution(6925542227628382171)
XLA Ops:
  0.6 0.0 copy-start
  0.6 0.0 copy-start.4
  0.7 1.9 %constant_dynamic-slice_fusion.2 = f32[256,512]{1,0:T(8,128)} fusion(f32[4096,512]{1,0:T(8,128)} %bitcast.16, s32[]{:T(128)S(6)} %select_n.13), kind=kLoop, calls=%fused_computation.3 | loop fusion | bytes 1048580 | tf_op jit(solution)/shard_map/dynamic_slice | solution.py:256
  2.5 10.0 %all-to-all-start = ((f32[16,16,512]{2,1,0:T(8,128)}), f32[16,16,512]{2,1,0:T(8,128)S(1)}, u32[]{:S(2)}, u32[]{:S(2)}) async-start(f32[16,16,512]{2,1,0:T(8,128)} %bitcast.1), calls=%async_computation | async-start | bytes 1048576 | tf_op jit(solution)/shard_map/all_to_all | solution.py:257
  12.6 0.0 copy-done
  12.6 0.7 constant_dynamic-slice_fusion.3
  14.5 0.0 copy-done.4
  14.6 0.1 dynamic_slice.19
  14.6 0.1 stack.31.place_ref.refs_0_
  14.7 1.8 %constant_dynamic-slice_fusion.own_ref = f32[2,512,512]{2,1,0:T(8,128)S(1)} fusion(f32[8,512,512]{2,1,0:T(8,128)} %param.4, s32[]{:T(128)S(6)} %select_n.15), kind=kLoop, calls=%fused_computation.1 | loop fusion | bytes 4194308 | tf_op jit(solution)/shard_map/dynamic_slice | solution.py:275
  16.5 0.9 halves.1.refs_2_.own_ref
  17.4 8.9 %all-to-all-done.mixed_ref = f32[16,16,512]{2,1,0:T(8,128)S(1)} async-done(((f32[16,16,512]{2,1,0:T(8,128)}), f32[16,16,512]{2,1,0:T(8,128)S(1)}, u32[]{:S(2)}, u32[]{:S(2)}) %all-to-all-start) | async-done | bytes 524320 | tf_op jit(solution)/shard_map/all_to_all | solution.py:257
  26.3 0.0 copy-start.3
  26.3 0.6 pick.1
  27.0 29.9 %all_to_all.15.both_ref = f32[16,32,512]{2,1,0:T(8,128)S(1)} all-to-all(f32[16,32,512]{2,1,0:T(8,128)S(1)} %pick.1), channel_id=1, replica_groups=mesh['occ'=16,'virt'=16] {'occ'}, dimensions={0} | all-to-all | bytes 2097152 | tf_op jit(solution)/shard_map/all_to_all | solution.py:282
  56.8 1.1 cut.1
  57.9 0.0 copy-start.1
  58.0 0.8 copy-done.1
  58.7 3.2 %collective-permute-start.2 = (f32[2,256,512]{2,1,0:T(8,128)}, f32[2,256,512]{2,1,0:T(8,128)}, u32[]{:S(2)}, u32[]{:S(2)}) collective-permute-start(f32[2,256,512]{2,1,0:T(8,128)} %get-tuple-element.22), channel_id=1, source_target_pairs={{0,1},{1,0},{2,3},{3,2},{4,5},{5,4},{6,7},{7,6},{8,9},{9,8},{10,11... | collective-permute-start | bytes 3145736 | tf_op jit(solution)/shard_map/ppermute | solution.py:26
  61.9 0.1 copy.6.refs_7_
  62.1 1.4 %collective-permute-start = (f32[256,512]{1,0:T(8,128)}, f32[256,512]{1,0:T(8,128)S(1)}, u32[]{:S(2)}, u32[]{:S(2)}) collective-permute-start(f32[256,512]{1,0:T(8,128)} %copy-done.1), channel_id=1, source_target_pairs={{0,2},{1,3},{2,0},{3,1},{4,6},{5,7},{6,4},{7,5},{8,10},{9,11},{10,... | collective-permute-start | bytes 1572872 | tf_op jit(solution)/shard_map/ppermute | solution.py:26
  63.5 1.9 %collective-permute-start.1 = (f32[256,512]{1,0:T(8,128)S(1)}, f32[256,512]{1,0:T(8,128)S(1)}, u32[]{:S(2)}, u32[]{:S(2)}) collective-permute-start(f32[256,512]{1,0:T(8,128)S(1)} %get-tuple-element.21.refs_5_), channel_id=1, source_target_pairs={{0,6},{1,7},{2,4},{3,5},{4,2},{5,3},{6,0},{7,1},{8,14},{9,15},{10,... | collective-permute-start | bytes 1572872 | tf_op jit(solution)/shard_map/ppermute | solution.py:26
  65.4 0.0 collective-permute-done.2.refs_4_.refs_6_
  65.4 0.0 copy-done.3
  65.4 0.0 copy-start.2
  65.4 1.0 copy-done.2
  66.4 8.6 %unit.2 = (f32[2,512,512]{2,1,0:T(8,128)S(1)}, f32[4,8,128]{2,1,0:T(8,128)S(1)}) custom-call(s32[7]{0:T(128)S(1)} %stack.31.place_ref.refs_0_, f32[128]{0:T(128)S(1)} %copy-done.3, bf16[2,1024,512]{2,1,0:T(8,128)(2,1)S(1)} %halves.1.refs_2_.own_ref, f32[256,512]{1,0:T(8,128)S(1)} %copy-done.2, f32[2,256,512]{2,1,0:T(8,128)} %collective-permute-done.2.refs_4_.refs_6_, ...), custom_call_target="tpu_custom_call" | custom-call | flops 6442450944 | bytes 4194304 | tf_op jit(solution)/shard_map/unit/pallas_call | solution.py:46
  75.0 0.9 collective-permute-done.refs_0_.refs_3_
  75.9 2.0 %collective-permute-done.1.refs_1_.refs_5_ = f32[256,512]{1,0:T(8,128)S(1)} collective-permute-done((f32[256,512]{1,0:T(8,128)S(1)}, f32[256,512]{1,0:T(8,128)S(1)}, u32[]{:S(2)}, u32[]{:S(2)}) %collective-permute-start.1) | collective-permute-done | bytes 524320 | tf_op jit(solution)/shard_map/ppermute | solution.py:26
  77.9 1.1 collective-permute-start.3
  79.0 0.0 collective-permute-start.4
  79.0 1.8 %near.1.refs_9_ = f32[4,512,256]{2,1,0:T(8,128)S(1)} custom-call(bf16[2,1024,512]{2,1,0:T(8,128)(2,1)S(1)} %halves.1.refs_2_.own_ref, f32[256,512]{1,0:T(8,128)S(1)} %collective-permute-done.refs_0_.refs_3_, f32[256,512]{1,0:T(8,128)S(1)} %collective-permute-done.1.refs_1_.refs_5_), custom_call_target="tpu_custom_call" | custom-call | flops 1610612736 | bytes 1048576 | tf_op jit(solution)/shard_map/near/pallas_call | solution.py:46
  80.8 0.0 collective-permute-done.3.refs_4_
  80.8 0.4 collective-permute-done.4.refs_6_
  81.3 6.1 %unit.3 = f32[16,264,128]{2,1,0:T(8,128)S(1)} custom-call(s32[7]{0:T(128)S(1)} %stack.31.place_ref.refs_0_, f32[128]{0:T(128)S(1)} %copy-done.3, bf16[2,1024,512]{2,1,0:T(8,128)(2,1)S(1)} %halves.1.refs_2_.own_ref, f32[256,512]{1,0:T(8,128)S(1)} %collective-permute-done.refs_0_.refs_3_, f32[256,512]{1,0:T(8,128)S(1)} %collective-permute-done.3.refs_4_, ...), custom_call_target="tpu_custom_call" | custom-call | flops 6442450944 | bytes 4194304 | tf_op jit(solution)/shard_map/unit/pallas_call | solution.py:46
  87.4 35.4 %all_to_all.16.slabs_ref = f32[16,264,128]{2,1,0:T(8,128)S(1)} all-to-all(f32[16,264,128]{2,1,0:T(8,128)S(1)} %unit.3), channel_id=1, replica_groups=mesh['occ'=16,'virt'=16] {'virt'}, dimensions={0} | all-to-all | bytes 4325376 | tf_op jit(solution)/shard_map/all_to_all | solution.py:305
  122.8 1.6 %finish.1 = (f32[8,32,512]{2,1,0:T(8,128)}, f32[2,8]{1,0:T(2,128)}) custom-call(f32[16,264,128]{2,1,0:T(8,128)S(1)} %all_to_all.16.slabs_ref), custom_call_target="tpu_custom_call" | custom-call | tf_op jit(solution)/shard_map/finish/pallas_call | solution.py:236
  (1 shorter events, 0.0 us)
Async XLA Ops:
  0.6 12.0 %copy-start = (s32[2,16]{1,0:T(2,128)S(1)}, s32[2,16]{1,0:T(2,128)}, u32[]{:S(2)}) copy-start(s32[2,16]{1,0:T(2,128)} %mates_ref.1) | copy-start | bytes 388
  0.6 13.9 %copy-start.4 = (f32[512]{0:T(512)S(1)}, f32[512]{0:T(512)}, u32[]{:S(2)}) copy-start(f32[512]{0:T(512)} %param.6) | copy-start | bytes 6148
  2.5 23.8 %all-to-all-start = ((f32[16,16,512]{2,1,0:T(8,128)}), f32[16,16,512]{2,1,0:T(8,128)S(1)}, u32[]{:S(2)}, u32[]{:S(2)}) async-start(f32[16,16,512]{2,1,0:T(8,128)} %bitcast.1), calls=%async_computation | async-start | bytes 1048576 | tf_op jit(solution)/shard_map/all_to_all | solution.py:257
  26.3 39.0 %copy-start.3 = (f32[128]{0:T(128)S(1)}, f32[128]{0:T(128)}, u32[]{:S(2)}) copy-start(f32[128]{0:T(128)} %refs_1_.3) | copy-start | bytes 1540
  57.9 0.8 copy-start.1
  58.7 6.6 %collective-permute-start.2 = (f32[2,256,512]{2,1,0:T(8,128)}, f32[2,256,512]{2,1,0:T(8,128)}, u32[]{:S(2)}, u32[]{:S(2)}) collective-permute-start(f32[2,256,512]{2,1,0:T(8,128)} %get-tuple-element.22), channel_id=1, source_target_pairs={{0,1},{1,0},{2,3},{3,2},{4,5},{5,4},{6,7},{7,6},{8,9},{9,8},{10,11... | collective-permute-start | bytes 3145736 | tf_op jit(solution)/shard_map/ppermute | solution.py:26
  62.1 13.9 %collective-permute-start = (f32[256,512]{1,0:T(8,128)}, f32[256,512]{1,0:T(8,128)S(1)}, u32[]{:S(2)}, u32[]{:S(2)}) collective-permute-start(f32[256,512]{1,0:T(8,128)} %copy-done.1), channel_id=1, source_target_pairs={{0,2},{1,3},{2,0},{3,1},{4,6},{5,7},{6,4},{7,5},{8,10},{9,11},{10,... | collective-permute-start | bytes 1572872 | tf_op jit(solution)/shard_map/ppermute | solution.py:26
  63.5 14.4 %collective-permute-start.1 = (f32[256,512]{1,0:T(8,128)S(1)}, f32[256,512]{1,0:T(8,128)S(1)}, u32[]{:S(2)}, u32[]{:S(2)}) collective-permute-start(f32[256,512]{1,0:T(8,128)S(1)} %get-tuple-element.21.refs_5_), channel_id=1, source_target_pairs={{0,6},{1,7},{2,4},{3,5},{4,2},{5,3},{6,0},{7,1},{8,14},{9,15},{10,... | collective-permute-start | bytes 1572872 | tf_op jit(solution)/shard_map/ppermute | solution.py:26
  65.4 1.0 copy-start.2
  77.9 2.9 %collective-permute-start.3 = (f32[256,512]{1,0:T(8,128)S(1)}, f32[256,512]{1,0:T(8,128)S(1)}, u32[]{:S(2)}, u32[]{:S(2)}) collective-permute-start(f32[256,512]{1,0:T(8,128)S(1)} %collective-permute-done.refs_0_.refs_3_), channel_id=1, source_target_pairs={{0,1},{1,0},{2,3},{3,2},{4,5},{5,4},{6,7},{7,6},{8,9},{9,8},{10,11... | collective-permute-start | bytes 1572872 | tf_op jit(solution)/shard_map/ppermute | solution.py:26
  79.0 2.3 %collective-permute-start.4 = (f32[256,512]{1,0:T(8,128)S(1)}, f32[256,512]{1,0:T(8,128)S(1)}, u32[]{:S(2)}, u32[]{:S(2)}) collective-permute-start(f32[256,512]{1,0:T(8,128)S(1)} %collective-permute-done.1.refs_1_.refs_5_), channel_id=1, source_target_pairs={{0,1},{1,0},{2,3},{3,2},{4,5},{5,4},{6,7},{7,6},{8,9},{9,8},{10,11... | collective-permute-start | bytes 1572872 | tf_op jit(solution)/shard_map/ppermute | solution.py:26
